TPU v7x, 512 devices: a whole 4x8x8 slice. The times are simulated.
512 devices in a mesh: gx: 32 (over z, x), gy: 16 (over y, core).
Axes of the slice: x: 4, y: 8, z: 8, core: 2. Of those that a mesh axis runs over, the one named last changes fastest.
Arguments:
- state: float32 [5, 16, 256, 2048], P(None, None, 'gx', 'gy'), may hold values from -3 to 60, as said below
- counts: int32 [5, 1, 32, 256], P(None, None, 'gx', 'gy'), may hold values from 1 to 15, as said below
- aggregator: int32 [32], P('gx'), may hold values from 0 to 15
Outputs:
- advanced: float32 [5, 8, 256, 2048], P(None, None, 'gx', 'gy')
- snapshot: float32 [32, 16, 10240], P('gx', 'gy')
Inputs may be any that keep to these rules, and one draw needn't show every extreme that they name: state has positive density and pressure. `counts`: the blocks of one x tile and one y tile keep at most 80 * (13) and at least 80 * (3) coefficients in all, and some y tile of every x tile keeps exactly the most; the blocks of one x tile keep exactly 10240 together.
All inputs are finite; a program needn't handle non-finite values.
Results may differ from a plain program's by a relative error of at most 0.0003.
Values sent between devices are 32-bit elements; how exact they have to be, the bound alone decides.
A program may use at most 64 MiB of HBM per device.

v0:
```python
import math

import jax
import jax.numpy as jnp
import numpy as np
from jax import lax
from jax.sharding import PartitionSpec as P

Z = 8
KEEP = 8
SKEW = 5


GAMMA = 1.4
COURANT = 0.1


def extended(cells, sides, width):
    for axis, dim in sides:
        count = lax.axis_size(axis)
        head = lax.slice_in_dim(cells, 0, width, axis=dim)
        tail = lax.slice_in_dim(cells, cells.shape[dim] - width, cells.shape[dim], axis=dim)
        cells = jnp.concatenate(
            [
                lax.ppermute(tail, axis, [(i, (i + 1) % count) for i in range(count)]),
                cells,
                lax.ppermute(head, axis, [((i + 1) % count, i) for i in range(count)]),
            ],
            axis=dim,
        )
    return cells


def minmod(slope_one, slope_two):
    return (
        0.5
        * (jnp.sign(slope_one) + jnp.sign(slope_two))
        * jnp.minimum(jnp.abs(slope_one), jnp.abs(slope_two))
    )


def primitive(conserved):
    density = conserved[0]
    velocity = conserved[1:4] / density
    pressure = (GAMMA - 1.0) * (conserved[4] - 0.5 * jnp.sum(conserved[1:4] * velocity, axis=0))
    return jnp.concatenate([density[None], velocity, pressure[None]], axis=0)


def face_terms(prims, component):
    density = prims[0]
    velocity = prims[1:4]
    pressure = prims[4]
    normal_speed = velocity[component]
    energy = pressure / (GAMMA - 1.0) + 0.5 * density * jnp.sum(velocity * velocity, axis=0)
    conserved = jnp.concatenate([density[None], density * velocity, energy[None]], axis=0)
    rows = [density * normal_speed]
    for index in range(3):
        term = density * velocity[index] * normal_speed
        if index == component:
            term = term + pressure
        rows.append(term)
    rows.append((energy + pressure) * normal_speed)
    fluxes = jnp.stack(rows, axis=0)
    signal = jnp.abs(normal_speed) + jnp.sqrt(GAMMA * pressure / density)
    return (conserved, fluxes, signal)


def axis_term(prims, spatial, component):
    length = prims.shape[spatial]

    def cut(start, stop):
        return lax.slice_in_dim(prims, start, stop, axis=spatial)

    centres = cut(1, length - 1)
    slopes = minmod(centres - cut(0, length - 2), cut(2, length) - centres)
    state_left = lax.slice_in_dim(centres + 0.5 * slopes, 0, length - 3, axis=spatial)
    state_right = lax.slice_in_dim(centres - 0.5 * slopes, 1, length - 2, axis=spatial)
    cons_left, flux_left, signal_left = face_terms(state_left, component)
    cons_right, flux_right, signal_right = face_terms(state_right, component)
    dissipation = jnp.maximum(signal_left, signal_right)
    fluxes = 0.5 * (flux_left + flux_right) - 0.5 * dissipation * (cons_right - cons_left)
    return lax.slice_in_dim(fluxes, 1, length - 3, axis=spatial) - lax.slice_in_dim(
        fluxes, 0, length - 4, axis=spatial
    )


def tendency(padded):
    prims = primitive(padded)
    along_z = axis_term(prims[:, :, 2:-2, 2:-2], 1, 2)
    along_x = axis_term(prims[:, 2:-2, :, 2:-2], 2, 0)
    along_y = axis_term(prims[:, 2:-2, 2:-2, :], 3, 1)
    return -(along_z + along_x + along_y)


def wave_max(conserved):
    prims = primitive(conserved)
    sound = jnp.sqrt(GAMMA * prims[4] / prims[0])
    return jnp.max(jnp.max(jnp.abs(prims[1:4]), axis=0) + sound)


def cosine_table():
    sample = jnp.arange(8, dtype=jnp.float32)
    freq = sample[:, None]
    table = jnp.cos(math.pi * (2.0 * sample[None, :] + 1.0) * freq / 16.0)
    weights = jnp.where(freq == 0, math.sqrt(0.125), 0.5)
    return table * weights


def rank_order():
    flat = np.arange(512)
    level = flat // 64 + flat // 8 % 8 + flat % 8
    keys = level * 512 + flat
    return np.argsort(keys, kind="stable").astype(np.int32)


def encode(fields):
    table = cosine_table()
    nfield, planes, xcells, ycells = fields.shape
    blocks = fields.reshape(nfield, planes // 8, 8, xcells // 8, 8, ycells // 8, 8)
    trans = jnp.einsum("kz,fazbxcy->fakbxcy", table, blocks, precision=lax.Precision.HIGHEST)
    trans = jnp.einsum("lx,fakbxcy->fakblcy", table, trans, precision=lax.Precision.HIGHEST)
    trans = jnp.einsum("my,fakblcy->fakblcm", table, trans, precision=lax.Precision.HIGHEST)
    trans = trans.transpose(0, 1, 3, 5, 2, 4, 6).reshape(
        nfield, planes // 8, xcells // 8, ycells // 8, 512
    )
    return trans[..., rank_order()]


def step_size(state):
    margin_planes = (state.shape[1] - Z) // 2
    local_top = wave_max(state[:, margin_planes : margin_planes + Z])
    return COURANT / lax.pmax(local_top, ("gx", "gy"))


def first_change(state, padded):
    step_ratio = step_size(state)
    change = tendency(padded)
    return (change, step_ratio)


def shards(state, counts, aggregator):
    margin_planes = (state.shape[1] - Z) // 2
    padded = extended(state, (("gx", 2), ("gy", 3)), 2)
    change, step_ratio = first_change(state, padded)
    section_one = state[:, 2:-2] + step_ratio * change
    padded_next = extended(section_one, (("gx", 2), ("gy", 3)), 2)
    second_core = section_one[:, 2:-2]
    change_next = tendency(padded_next)
    advanced = 0.5 * state[:, margin_planes : margin_planes + Z] + 0.5 * (
        second_core + step_ratio * change_next
    )
    coded = encode(advanced)
    blocks_dev = coded.shape[0] * coded.shape[1] * coded.shape[2] * coded.shape[3]
    dev_cap = blocks_dev * (KEEP + SKEW)
    values = coded.reshape(blocks_dev, 512)
    kept = counts.reshape(blocks_dev)
    offsets = jnp.cumsum(kept) - kept
    rank_index = jnp.arange(512, dtype=jnp.int32)
    is_kept = rank_index[None, :] < kept[:, None]
    targets = jnp.where(is_kept, offsets[:, None] + rank_index[None, :], dev_cap).astype(jnp.int32)
    stream = (
        jnp.zeros((dev_cap,), jnp.float32)
        .at[targets.reshape(-1)]
        .set(values.reshape(-1), mode="drop")
    )
    totals = jnp.sum(kept).astype(jnp.float32).reshape(1)
    group_size = lax.axis_size("gy")
    group_cap = group_size * blocks_dev * KEEP
    leader = aggregator[0]
    all_streams, all_totals = (
        lax.all_gather(stream[None], "gy", axis=0, tiled=True),
        lax.all_gather(totals, "gy", axis=0, tiled=True),
    )
    dev_totals = all_totals.astype(jnp.int32)
    turn_rank = (jnp.arange(group_size, dtype=jnp.int32) - leader) % group_size
    earlier = (turn_rank[None, :] < turn_rank[:, None]).astype(jnp.int32)
    dev_offsets = jnp.sum(earlier * dev_totals[None, :], axis=1)
    slot_index = jnp.arange(dev_cap, dtype=jnp.int32)
    placed = jnp.where(
        slot_index[None, :] < dev_totals[:, None],
        dev_offsets[:, None] + slot_index[None, :],
        group_cap,
    ).astype(jnp.int32)
    group_stream = (
        jnp.zeros((group_cap,), jnp.float32)
        .at[placed.reshape(-1)]
        .set(all_streams.reshape(-1), mode="drop")
    )
    my_index = lax.axis_index("gy")
    snapshot = jnp.where(my_index == leader, group_stream, jnp.zeros((), jnp.float32)).reshape(
        1, 1, group_cap
    )
    return (advanced, snapshot)


def solution(mesh):
    placed = (P(None, None, "gx", "gy"), P(None, None, "gx", "gy"), P("gx"))
    return jax.shard_map(
        shards,
        mesh=mesh,
        in_specs=placed,
        out_specs=(P(None, None, "gx", "gy"), P("gx", "gy", None)),
        check_vma=False,
    )
```

profile of v0, /device:TPU:1, one launch (start us, length us, event | category | flops | bytes accessed | tf_op | source)
XLA Modules:
  0.0 552.3 jit_solution(14189647283481315745)
XLA Ops:
  8.4 3.9 collective-permute-start
  12.3 11.8 %collective-permute-start.1 = (f32[5,16,2,128]{3,1,2,0:T(8,128)S(1)}, f32[5,16,2,128]{3,1,2,0:T(8,128)S(1)}, u32[]{:S(2)}, u32[]{:S(2)}) collective-permute-start(f32[5,16,2,128]{3,1,2,0:T(8,128)S(1)} %copy.247), channel_id=1, source_target_pairs={{16,0},{32,16},{48,32},{64,48},{80,64},{96,80},{112,96},{128,112},... | collective-permute-start | bytes 245768 | tf_op jit(solution)/shard_map/ppermute | solution.py:27
  24.1 4.0 copy.219
  32.4 24.5 %all-reduce = f32[16]{0:T(128)S(1)} all-reduce(f32[16]{0:T(128)S(1)} %dynamic-update-slice), channel_id=1, replica_groups=mesh['gx'=32,'gy'=16] {'gy'}, use_global_device_ids=true, to_apply=%add | all-reduce | flops 16 | bytes 128
  58.4 3.2 copy.218
  61.6 3.2 copy.220
  64.8 8.3 %pad_maximum_fusion = f32[5,16,12,128]{2,1,3,0:T(8,128)S(1)} fusion(f32[5,16,2,128]{2,1,3,0:T(8,128)} %copy.220, f32[5,16,8,128]{2,1,3,0:T(8,128)} %copy.219, f32[5,16,2,128]{2,1,3,0:T(8,128)} %copy.218), kind=kLoop, calls=%fused_computation.3 | loop fusion | flops 245760 | bytes 983040 | tf_op jit(solution)/shard_map/concatenate | solution.py:23
  73.1 2.3 copy-done
  76.2 1.9 collective-permute-start.3
  78.1 95.9 %pmax.7 = f32[]{:T(128)} all-reduce(f32[]{:T(128)} %fusion.83), channel_id=1, replica_groups=mesh['gx'=32,'gy'=16] {'gx','gy'}, use_global_device_ids=true, to_apply=%region_3.0 | all-reduce | flops 1 | bytes 8 | tf_op jit(solution)/shard_map/pmax | solution.py:132
  174.7 3.3 copy.222
  186.2 3.6 collective-permute-start.4
  189.9 5.2 collective-permute-start.5
  196.6 1.8 collective-permute-start.6
  199.3 4.9 collective-permute-done.6
  204.2 2.8 collective-permute-done.7
  212.9 2.1 copy.240
  215.0 2.5 convolution_bitcast_fusion.1
  217.6 2.0 convolution_bitcast_fusion
  220.9 2.2 copy.243
  223.0 2.6 gather_fusion
  226.1 149.9 %scatter_custom_fusion = f32[1040]{0:T(1024)S(1)} fusion(s32[40960]{0:T(1024)S(1)} %bitcast.169, f32[40960]{0:T(1024)S(1)} %bitcast.170, f32[]{:T(128)} %constant.32.clone.1), kind=kCustom, calls=%fused_computation.288 | custom fusion | bytes 4164 | tf_op jit(solution)/shard_map/scatter | solution.py:164
  377.2 106.0 %all-reduce.4.cloned.1.call-done = f32[16640]{0:T(1024)} async-done(((f32[16640]{0:T(1024)}), f32[16640]{0:T(1024)}) %all-reduce.4.cloned.1.call-update) | async-done | bytes 66576
  483.3 61.5 %scatter_custom_fusion.1 = f32[10240]{0:T(1024)S(1)} fusion(s32[16640]{0:T(1024)S(1)} %fusion.54, f32[16640]{0:T(1024)} %all-reduce.4.cloned.1.call-done, f32[]{:T(128)} %constant.32.clone.1), kind=kCustom, calls=%fused_computation.280 | custom fusion | bytes 41472 | tf_op jit(solution)/shard_map/scatter | solution.py:187
  (165 shorter events, 25.3 us)
Async XLA Ops:
  7.2 476.1 %all-reduce.4.cloned.1.call-start = ((), (), s32[]{:S(2)}) async-start(), calls=%async_computation | async-start | bytes 139264
  8.4 50.0 %collective-permute-start = (f32[5,16,2,128]{3,1,2,0:T(8,128)S(1)}, f32[5,16,2,128]{3,1,2,0:T(8,128)S(1)}, u32[]{:S(2)}, u32[]{:S(2)}) collective-permute-start(f32[5,16,2,128]{3,1,2,0:T(8,128)S(1)} %copy.246), channel_id=1, source_target_pairs={{0,16},{16,32},{32,48},{48,64},{64,80},{80,96},{96,112},{112,128},... | collective-permute-start | bytes 245768 | tf_op jit(solution)/shard_map/ppermute | solution.py:25
  12.3 15.8 %copy-start.1 = (f32[5,16,8,128]{3,2,1,0:T(8,128)S(1)}, f32[5,16,8,128]{3,2,1,0:T(8,128)}, u32[]{:S(2)}) copy-start(f32[5,16,8,128]{3,2,1,0:T(8,128)} %param.5) | copy-start | bytes 983044
  12.3 15.8 %copy-start.4 = (s32[5,1,1,16]{3,2,1,0:T(1,128)S(1)}, s32[5,1,1,16]{3,2,1,0:T(1,128)}, u32[]{:S(2)}) copy-start(s32[5,1,1,16]{3,2,1,0:T(1,128)} %param.6) | copy-start | bytes 964
  12.3 49.2 %collective-permute-start.1 = (f32[5,16,2,128]{3,1,2,0:T(8,128)S(1)}, f32[5,16,2,128]{3,1,2,0:T(8,128)S(1)}, u32[]{:S(2)}, u32[]{:S(2)}) collective-permute-start(f32[5,16,2,128]{3,1,2,0:T(8,128)S(1)} %copy.247), channel_id=1, source_target_pairs={{16,0},{32,16},{48,32},{64,48},{80,64},{96,80},{112,96},{128,112},... | collective-permute-start | bytes 245768 | tf_op jit(solution)/shard_map/ppermute | solution.py:27
  73.1 2.3 copy-start
  75.4 102.6 %collective-permute-start.2 = (f32[5,16,12,2]{2,1,3,0:T(8,128)S(1)}, f32[5,16,12,2]{2,1,3,0:T(8,128)S(1)}, u32[]{:S(2)}, u32[]{:S(2)}) collective-permute-start(f32[5,16,12,2]{2,1,3,0:T(8,128)S(1)} %get-tuple-element.40), channel_id=1, source_target_pairs={{0,1},{1,2},{2,3},{3,4},{4,5},{5,6},{6,7},{7,8},{8,9},{9,10},{10,1... | collective-permute-start | bytes 23048 | tf_op jit(solution)/shard_map/ppermute | solution.py:25
  76.2 102.5 %collective-permute-start.3 = (f32[5,16,12,2]{2,1,3,0:T(8,128)S(1)}, f32[5,16,12,2]{2,1,3,0:T(8,128)S(1)}, u32[]{:S(2)}, u32[]{:S(2)}) collective-permute-start(f32[5,16,12,2]{2,1,3,0:T(8,128)S(1)} %get-tuple-element.41), channel_id=1, source_target_pairs={{1,0},{2,1},{3,2},{4,3},{5,4},{6,5},{7,6},{8,7},{9,8},{10,9},{11,1... | collective-permute-start | bytes 23048 | tf_op jit(solution)/shard_map/ppermute | solution.py:27
  185.8 9.2 %copy-start.5 = (s32[512]{0:T(512)S(1)}, s32[512]{0:T(512)}, u32[]{:S(2)}) copy-start(s32[512]{0:T(512)} %constant.56) | copy-start | bytes 6148
  186.2 8.9 %collective-permute-start.4 = (f32[5,12,2,128]{3,1,2,0:T(8,128)S(1)}, f32[5,12,2,128]{3,1,2,0:T(8,128)S(1)}, u32[]{:S(2)}, u32[]{:S(2)}) collective-permute-start(f32[5,12,2,128]{3,1,2,0:T(8,128)S(1)} %copy.235), channel_id=1, source_target_pairs={{0,16},{16,32},{32,48},{48,64},{64,80},{80,96},{96,112},{112,128},... | collective-permute-start | bytes 184328 | tf_op jit(solution)/shard_map/ppermute | solution.py:25
  189.9 6.4 %collective-permute-start.5 = (f32[5,12,2,128]{3,1,2,0:T(8,128)S(1)}, f32[5,12,2,128]{3,1,2,0:T(8,128)S(1)}, u32[]{:S(2)}, u32[]{:S(2)}) collective-permute-start(f32[5,12,2,128]{3,1,2,0:T(8,128)S(1)} %copy.236), channel_id=1, source_target_pairs={{16,0},{32,16},{48,32},{64,48},{80,64},{96,80},{112,96},{128,112},... | collective-permute-start | bytes 184328 | tf_op jit(solution)/shard_map/ppermute | solution.py:27
  196.6 7.5 %collective-permute-start.6 = (f32[5,12,12,2]{3,2,1,0:T(8,128)S(1)}, f32[5,12,12,2]{3,2,1,0:T(8,128)S(1)}, u32[]{:S(2)}, u32[]{:S(2)}) collective-permute-start(f32[5,12,12,2]{3,2,1,0:T(8,128)S(1)} %get-tuple-element.60), channel_id=1, source_target_pairs={{0,1},{1,2},{2,3},{3,4},{4,5},{5,6},{6,7},{7,8},{8,9},{9,10},{10,1... | collective-permute-start | bytes 17288 | tf_op jit(solution)/shard_map/ppermute | solution.py:25
  198.4 8.6 %collective-permute-start.7 = (f32[5,12,12,2]{3,2,1,0:T(8,128)S(1)}, f32[5,12,12,2]{3,2,1,0:T(8,128)S(1)}, u32[]{:S(2)}, u32[]{:S(2)}) collective-permute-start(f32[5,12,12,2]{3,2,1,0:T(8,128)S(1)} %get-tuple-element.61), channel_id=1, source_target_pairs={{1,0},{2,1},{3,2},{4,3},{5,4},{6,5},{7,6},{8,7},{9,8},{10,9},{11,1... | collective-permute-start | bytes 17288 | tf_op jit(solution)/shard_map/ppermute | solution.py:27
  211.5 3.5 copy-start.2
  376.4 0.6 copy-start.3
Sparse Core Ops, SparseCore 0:
  377.1 106.0 all-reduce.3
where the time goes:
time: 553 us; the launch traced here: 552 us
  local copies, waits for them, and re-layouts  243 us (44%)
  blocking collectives  120 us (22%)
  waiting for transfers between devices  115 us (21%)
  starting transfers between devices  29.1 us (5%)
  other arithmetic  21.2 us (4%)
  between operations  17.7 us (3%)
  matrix products  5.85 us (1%)
    scatter x1, local copies, waits for them, and re-layouts, shards(): stream = jnp.zeros((dev_cap,), jnp.float32).at[targets.reshape(-1)].set(v...  150 us
    unnamed x2, waiting for transfers between devices  106 us
    pmax x1, blocking collectives, step_size(): return COURANT / lax.pmax(local_top, ('gx', 'gy'))  95.9 us
    scatter x1, local copies, waits for them, and re-layouts, shards(): group_stream = jnp.zeros((group_cap,), jnp.float32).at[placed.reshape(-1)...  61.5 us
    unnamed x1, blocking collectives  24.5 us
    ppermute x4, starting transfers between devices, extended(): lax.ppermute(head, axis, [((i + 1) % count, i) for i in range(count)])  18.9 us
  transfers between devices with their start and end apart: 9, of which 4 were waited for; matrix products, arithmetic and copies ran while one was open for 3% of the time, Pallas kernels for 0%

commit v1 on v0

v1 whole, which is shorter than its diff:
```python
import functools
import math

import jax
import jax.numpy as jnp
import numpy as np
from jax import lax
from jax.experimental import pallas as pl
from jax.experimental.pallas import tpu as pltpu
from jax.sharding import PartitionSpec as P

MESH = pl.DeviceIdType.MESH
F32 = jnp.float32
HIGHEST = lax.Precision.HIGHEST
GAMMA = 1.4
COURANT = 0.1
INNER = {32: 4, 4: 2}
PAIR = 2
CORNERS = [(0, -1), (0, 1), (1, -1), (-1, -1), (1, 1), (-1, 1)]
CHUNKS = [[((0, 0), 4), ((0, 1), 3), ((0, 3), 1)], [((0, 2), 2), ((1, 0), 3), ((1, 1), 1), ((2, 0), 1)]]
COMBOS = [c for chunk in CHUNKS for c, _ in chunk]


def cosine_np():
    k = np.arange(8)[:, None]
    n = np.arange(8)[None, :]
    w = np.where(k == 0, math.sqrt(0.125), 0.5)
    return np.cos(math.pi * (2 * n + 1) * k / 16.0) * w


def rank_of():
    flat = np.arange(512)
    keys = (flat // 64 + flat // 8 % 8 + flat % 8) * 512 + flat
    order = np.argsort(keys, kind="stable")
    rank = np.empty(512, np.int64)
    rank[order] = np.arange(512)
    return rank.reshape(8, 8, 8)


def tables():
    c = cosine_np()
    rank = rank_of()
    first = np.zeros((56, 320), np.float32)
    for i, (kz, kx) in enumerate(COMBOS):
        for f in range(5):
            first[i * 8 + f, f * 64 : f * 64 + 64] = np.outer(c[kz], c[kx]).reshape(64)
    second = np.zeros((len(COMBOS) * 128, 128), np.float32)
    ranks = np.full((2, 128), 1000, np.int32)
    row = 0
    for k, chunk in enumerate(CHUNKS):
        slot = 0
        for (kz, kx), n in chunk:
            for ky in range(n):
                for b in range(16):
                    second[row * 128 + b * 8 : row * 128 + b * 8 + 8, slot * 16 + b] = c[ky]
                ranks[k, slot * 16 : slot * 16 + 16] = rank[kz, kx, ky]
                slot += 1
            row += 1
    b = np.arange(16)[:, None]
    lane = np.arange(128)[None, :] % 16
    count = np.concatenate([(b < lane), (b == lane), np.ones((16, 128))], axis=1).astype(np.float32)
    return first, second, ranks, count


def half_slope(a, b):
    return 0.5 * (jnp.maximum(jnp.minimum(a, b), 0.0) + jnp.minimum(jnp.maximum(a, b), 0.0))


def prims_of(cons):
    rho, mx, my, mz, en = cons
    inv = 1.0 / rho
    u, v, w = mx * inv, my * inv, mz * inv
    p = (GAMMA - 1.0) * (en - 0.5 * (mx * u + my * v + mz * w))
    return [rho, u, v, w, p]


def side_terms(q, comp):
    rho, p = q[0], q[4]
    vel = q[1:4]
    vn = vel[comp]
    mom = [rho * x for x in vel]
    en = p * (1.0 / (GAMMA - 1.0)) + 0.5 * (mom[0] * vel[0] + mom[1] * vel[1] + mom[2] * vel[2])
    rows = [mom[comp]]
    for i in range(3):
        t = mom[i] * vn
        rows.append(t + p if i == comp else t)
    rows.append((en + p) * vn)
    return [rho] + mom + [en], rows, jnp.abs(vn) + jnp.sqrt(GAMMA * p / rho)


def flux2(left, right, comp):
    ul, fl, sl = side_terms(left, comp)
    ur, fr, sr = side_terms(right, comp)
    a = jnp.maximum(sl, sr)
    return [(x + y) - a * (d - c) for x, y, c, d in zip(fl, fr, ul, ur)]


def sub(a, b):
    return [x - y for x, y in zip(a, b)]


def add(a, b):
    return [x + y for x, y in zip(a, b)]


def rollto(x, shift, axis):
    n = x.shape[axis]
    shift %= n
    return pltpu.roll(x, shift, axis) if shift else x


def last(x):
    return x.ndim - 1


def iota(shape, dim):
    return lax.broadcasted_iota(jnp.int32, shape, dim)


def z_term(w):
    out_l, out_r = [], []
    for x in w:
        d = x[1:] - x[:-1]
        h = half_slope(d[1:], d[:-1])
        c = x[1:-1]
        out_l.append((c + h)[:-1])
        out_r.append((c - h)[1:])
    f = flux2(out_l, out_r, 2)
    return [x[1:] - x[:-1] for x in f]


def x_next(a, b):
    row = iota(a.shape, a.ndim - 2)
    return jnp.where(row == 7, rollto(b, -1, b.ndim - 2), rollto(a, -1, a.ndim - 2))


def x_prev(a, b):
    row = iota(a.shape, a.ndim - 2)
    return jnp.where(row == 0, rollto(b, 1, b.ndim - 2), rollto(a, 1, a.ndim - 2))


def x_terms(a, b):
    la, ra, lb, rb = [], [], [], []
    for x, y in zip(a, b):
        fx, fy = x_next(x, y) - x, x_next(y, x) - y
        hx, hy = half_slope(fx, x_prev(fx, fy)), half_slope(fy, x_prev(fy, fx))
        la.append(x + hx)
        lb.append(y + hy)
        wx, wy = x - hx, y - hy
        ra.append(x_next(wx, wy))
        rb.append(x_next(wy, wx))
    fa, fb = flux2(la, ra, 0), flux2(lb, rb, 0)
    ta = [x - x_prev(x, y) for x, y in zip(fa, fb)]
    tb = [y - x_prev(y, x) for x, y in zip(fa, fb)]
    return ta, tb


def y_term(w, e1, e2):
    lane = iota(w[0].shape, last(w[0]))
    left, right = [], []
    for x, e, g in zip(w, e1, e2):
        nxt = jnp.where(lane == 127, e, rollto(x, -1, last(x)))
        prv = jnp.where(lane == 0, e, rollto(x, 1, last(x)))
        h = half_slope(nxt - x, x - prv)
        left.append(x + h)
        right.append(jnp.where(lane == 127, g, rollto(x - h, -1, last(x))))
    f = flux2(left, right, 1)
    return [x - jnp.where(lane == 0, g, rollto(x, 1, last(x))) for x, g in zip(f, e2)]


def packed_y(w):
    left, right = [], []
    for x in w:
        d = rollto(x, -1, last(x)) - x
        h = half_slope(d, rollto(d, 1, last(d)))
        left.append(x + h)
        right.append(x - h)
    f = flux2(left, [rollto(x, -1, last(x)) for x in right], 1)
    return right, f


def packed_z(w):
    left, right = [], []
    for x in w:
        d = rollto(x, -8, last(x)) - x
        h = half_slope(d, rollto(d, 8, last(d)))
        left.append(x + h)
        right.append(x - h)
    f = flux2(left, [rollto(x, -8, last(x)) for x in right], 2)
    return [x - rollto(x, 8, last(x)) for x in f]


def edge_lanes(low, high):
    col = iota(low.shape, last(low)) % 8
    return jnp.where(col == 7, rollto(high, 3, last(high)), rollto(low, 5, last(low)))


def pack_columns(planes, zs):
    out = None
    for z in zs:
        r = rollto(planes(z), 8 * z + 4, 1)
        out = r if out is None else jnp.where(iota(r.shape, 1) // 8 == z, r, out)
    return out


def kernel(
    ngx, ngy, state, counts, agg, first, second, ranks, cmat,
    adv_out, snap_out,
    W, XH, L, Lx, Wx, E1, E2, E1x, E2x, sendx, recvx, qown, recvq, qx,
    maxsend, ry, rz, rx, tot, adv,
    ga, gb, sa, sb, gbrows, xedge, xinj,
    sem_hs, sem_hr, sem_qs, sem_qr, sem_ms, sem_mr, sem_as, sem_ar, sem_bs, sem_br,
):
    nx = INNER[ngx]
    nz = ngx // nx
    gx = lax.axis_index("gx")
    gy = lax.axis_index("gy")
    zc, xc = gx // nx, gx % nx

    def at(dx, dy):
        return ((gx + dx + ngx) % ngx, (gy + dy + ngy) % ngy)

    y_peers = [at(0, k) for k in range(1, ngy)]
    z_peers = [(((zc + k) % nz) * nx + xc, gy) for k in range(1, nz)]
    x_peers = [(zc * nx + (xc + k) % nx, gy) for k in range(1, nx)]
    halo_peers = [at(-1, 0), at(1, 0)]
    q_peers = [at(-dx, -dy) for dx, dy in CORNERS]

    barrier = pltpu.get_barrier_semaphore()
    everyone = y_peers + z_peers + x_peers + halo_peers + q_peers[2:]
    for peer in everyone:
        pl.semaphore_signal(barrier, inc=1, device_id=peer, device_id_type=MESH)

    vmax = None
    for z in range(16):
        w = prims_of([state[f, z] for f in range(5)])
        for f in range(5):
            W[f, z] = w[f]
        if 4 <= z < 12:
            c = jnp.sqrt(GAMMA * w[4] / w[0])
            s = jnp.maximum(jnp.maximum(jnp.abs(w[1]), jnp.abs(w[2])), jnp.abs(w[3])) + c
            vmax = s if vmax is None else jnp.maximum(vmax, s)
    top = jnp.max(jnp.max(vmax, axis=0, keepdims=True), axis=1, keepdims=True)

    cnt = jnp.zeros((8, 16), F32)
    row16 = iota((8, 16), 0)
    for f in range(5):
        cnt = jnp.where(row16 == f, counts[f, 0].astype(F32), cnt)
    cexp = jnp.dot(cnt, cmat[...], preferred_element_type=F32)
    total = jnp.sum(cexp[:, 256:384], axis=0, keepdims=True)
    lane1 = iota((1, 128), 1)
    maxsend[0] = jnp.where(lane1 < 64, top, total)
    ry[0] = maxsend[0]

    row8 = iota((8, 128), 0)
    for f in range(5):
        for k in range(6):
            lo, hi = state[f, 2 + k], state[f, 8 + k]
            sendx[0, f, k] = jnp.where(row8 < 4, lo, rollto(hi, 4, 0))
            sendx[1, f, k] = jnp.where(row8 < 4, rollto(lo, 4, 0), hi)
        qown[f] = pack_columns(lambda z: state[f, z], range(16))

    pl.semaphore_wait(barrier, len(everyone))

    def copies(src, bufs, peers, send, recv, base):
        return [
            pltpu.make_async_remote_copy(
                src_ref=src, dst_ref=bufs.at[k + 1], send_sem=send.at[base + k], recv_sem=recv.at[base + k],
                device_id=peer, device_id_type=MESH,
            )
            for k, peer in enumerate(peers)
        ]

    cy = copies(maxsend.at[0], ry, y_peers, sem_ms, sem_mr, 0)
    for c in cy:
        c.start()
    cq = [
        pltpu.make_async_remote_copy(
            src_ref=qown, dst_ref=recvq.at[i], send_sem=sem_qs.at[i], recv_sem=sem_qr.at[i],
            device_id=peer, device_id_type=MESH,
        )
        for i, peer in enumerate(q_peers)
    ]
    for c in cq:
        c.start()
    ch = [
        pltpu.make_async_remote_copy(
            src_ref=sendx.at[i], dst_ref=recvx.at[i], send_sem=sem_hs.at[i], recv_sem=sem_hr.at[i],
            device_id=peer, device_id_type=MESH,
        )
        for i, peer in enumerate(halo_peers)
    ]
    for c in ch:
        c.start()

    def load(ref, start, n):
        return [ref[f, pl.ds(start, n)] for f in range(5)]

    def z_main(i, carry):
        z0 = i * PAIR
        t = z_term(load(W, z0, PAIR + 4))
        for f in range(5):
            L[f, pl.ds(z0, PAIR)] = t[f]
        return carry

    lax.fori_loop(0, 12 // PAIR, z_main, 0)

    for c in cy:
        c.wait()
    best = ry[0]
    for k in range(ngy):
        if k:
            best = jnp.maximum(best, ry[k])
        tot[k : k + 1, :] = jnp.where(lane1 < 64, rollto(ry[k], 64, 1), ry[k])
    maxsend[1] = jnp.where(lane1 < 64, best, rollto(best, 64, 1))
    cz = copies(maxsend.at[1], rz, z_peers, sem_ms, sem_mr, ngy)
    for c in cz:
        c.start()

    for c in cq:
        c.wait()
    for c in ch:
        c.wait()
    for f in range(5):
        for k in range(6):
            a, b = recvx[0, f, k], recvx[1, f, k]
            XH[f, k] = jnp.where(row8 < 4, a, rollto(b, 4, 0))
            XH[f, k + 6] = jnp.where(row8 < 4, rollto(a, 4, 0), b)
    for z in range(12):
        w = prims_of([XH[f, z] for f in range(5)])
        for f in range(5):
            Wx[f, z] = w[f]
    colm = iota((8, 128), 1) % 8
    packed = []
    for f in range(5):
        q = qown[f]
        qh = pack_columns(lambda z: XH[f, z - 2], range(2, 14))
        lo = jnp.where(row8 < 4, recvq[2, f], recvq[3, f])
        hi = jnp.where(row8 < 4, recvq[4, f], recvq[5, f])
        packed.append(
            jnp.stack(
                [
                    jnp.where(colm < 4, recvq[0, f], q),
                    jnp.where(colm < 4, q, recvq[1, f]),
                    jnp.where(colm < 4, lo, qh),
                    jnp.where(colm < 4, qh, hi),
                ]
            )
        )
    pw = prims_of(packed)
    pr, pf = packed_y(pw)
    ta, _ = x_terms([x[:2] for x in pw], [x[2:] for x in pw])
    tz = packed_z([x[:2] for x in pw])
    for f in range(5):
        ty = pf[f] - rollto(pf[f], 1, 2)
        qx[0, f] = packed[f][:2]
        qx[1, f] = ta[f] + tz[f] + ty[:2]

    def inject(e1, e2, pw, pr, pf, low, high, planes, offset):
        for f in range(5):
            c1 = edge_lanes(pw[f][low], pw[f][high])
            c2 = edge_lanes(pf[f][low], pr[f][high])
            for z in planes:
                e1[f, z - offset] = rollto(c1, -(8 * z + 8), 1)
                e2[f, z - offset] = rollto(c2, -(8 * z + 8), 1)

    inject(E1, E2, pw, pr, pf, 0, 1, range(2, 14), 2)
    inject(E1x, E2x, pw, pr, pf, 2, 3, range(4, 12), 4)

    def xy_main(i, carry):
        z0 = i * PAIR
        a = load(W, z0 + 2, PAIR)
        ta, tb = x_terms(a, load(Wx, z0, PAIR))
        ty = y_term(a, load(E1, z0, PAIR), load(E2, z0, PAIR))
        for f in range(5):
            L[f, pl.ds(z0, PAIR)] = L[f, pl.ds(z0, PAIR)] + ta[f] + ty[f]
            Lx[f, pl.ds(z0, PAIR)] = tb[f]
        return carry

    lax.fori_loop(0, 12 // PAIR, xy_main, 0)

    for c in cz:
        c.wait()
    best = maxsend[1]
    for k in range(1, nz):
        best = jnp.maximum(best, rz[k])
    maxsend[2] = best
    cx = copies(maxsend.at[2], rx, x_peers, sem_ms, sem_mr, ngy + nz)
    for c in cx:
        c.start()

    def strip(i, carry):
        z0 = i * PAIR
        w = load(Wx, z0, PAIR + 4)
        tz = z_term(w)
        ty = y_term([x[2:-2] for x in w], load(E1x, z0, PAIR), load(E2x, z0, PAIR))
        for f in range(5):
            Lx[f, pl.ds(z0 + 2, PAIR)] = Lx[f, pl.ds(z0 + 2, PAIR)] + tz[f] + ty[f]
        return carry

    lax.fori_loop(0, 8 // PAIR, strip, 0)
    for f in range(5):
        for j, r in enumerate((6, 7, 0, 1)):
            for z in range(8):
                xedge[0, f, j, z : z + 1, :] = XH[f, z + 2, r : r + 1, :]
                xedge[1, f, j, z : z + 1, :] = Lx[f, z + 2, r : r + 1, :]
        for j, r in enumerate((0, 1, 7)):
            for z in range(8):
                xedge[0, f, j + 4, z : z + 1, :] = state[f, z + 4, r : r + 1, :]
                xedge[1, f, j + 4, z : z + 1, :] = L[f, z + 2, r : r + 1, :]

    me_rank = jnp.full((1, 1), (gy - agg[0] + ngy) % ngy, jnp.int32)
    nlane = ngy * 8
    slot_col = iota((ngy, nlane), 0)
    slot_row = iota((ngy, nlane), 1) // 8

    def turn(slot):
        return (gy - slot - agg[0] + 2 * ngy) & (ngy - 1)

    totals = tot[...]
    before = jnp.where(turn(slot_col) < turn(slot_row), totals[:, :nlane], 0.0)
    starts = jnp.sum(before, axis=0, keepdims=True).astype(jnp.int32)
    mine = jnp.sum(
        jnp.where(turn(iota((ngy, 128), 0)) < me_rank, totals, 0.0), axis=0, keepdims=True
    ).astype(jnp.int32)
    field_total = cexp[:, 256:384]
    upto = cexp[:, :128]
    for f in range(4):
        upto = upto + jnp.where(row8 > f, field_total[f : f + 1, :], 0.0)
    own_count = cexp[:, 128:256].astype(jnp.int32)
    base = upto.astype(jnp.int32) + (mine & 127)
    dest, spots = [], []
    for k in range(2):
        rank = ranks[k : k + 1, :]
        pos = base + rank
        keep = rank < own_count
        row_to = jnp.where(keep, pos >> 7, -1)
        lane_to = pos & 127
        for f in range(5):
            dest.append(row_to[f : f + 1, :])
            spots.append((iota((128, 128), 0) == lane_to[f : f + 1, :]).astype(F32))
    spots = jnp.concatenate(spots, axis=1)
    dest = [(iota((16, 128), 0) == d).astype(F32) for d in dest]

    for c in cx:
        c.wait()
    best = maxsend[2]
    for k in range(1, nx):
        best = jnp.maximum(best, rx[k])
    ratio = COURANT / best
    half = -0.5 * ratio

    p1 = prims_of([qx[0, f] + half * qx[1, f] for f in range(5)])
    pr, pf = packed_y(p1)
    inject(E1, E2, p1, pr, pf, 0, 1, range(4, 12), 4)
    we = prims_of([xedge[0, f] + half * xedge[1, f] for f in range(5)])
    fl, fr = [], []
    for f in range(5):
        m2, m1, p8, p9, c0, c1, c7 = [we[f][j] for j in range(7)]
        h = half_slope(c0 - m1, m1 - m2)
        g = half_slope(c1 - c0, c0 - m1)
        fl.append(m1 + h)
        fr.append(c0 - g)
        xinj[0, f] = m1
        xinj[1, f] = p8
        xinj[2, f] = p8 - half_slope(p9 - p8, p8 - c7)
    fx = flux2(fl, fr, 0)
    for f in range(5):
        xinj[3, f] = fx[f]

    def section(i, carry):
        z0 = i * PAIR
        s = [state[f, pl.ds(z0 + 2, PAIR)] + half * L[f, pl.ds(z0, PAIR)] for f in range(5)]
        w = prims_of(s)
        for f in range(5):
            L[f, pl.ds(z0, PAIR)] = s[f]
            W[f, pl.ds(z0, PAIR)] = w[f]
        return carry

    lax.fori_loop(0, 12 // PAIR, section, 0)

    def second_step(i, carry):
        z0 = i * PAIR
        w = load(W, z0, PAIR + 4)
        tz = z_term(w)
        c = [x[2:-2] for x in w]
        ty = y_term(c, load(E1, z0, PAIR), load(E2, z0, PAIR))

        def rows(j, f):
            return jnp.stack([xinj[j, f, pl.ds(z0 + d, 1), :] for d in range(PAIR)])

        row = iota(c[0].shape, 1)
        left, right, inj = [], [], []
        for f in range(5):
            x = c[f]
            nxt = jnp.where(row == 7, rows(1, f), rollto(x, -1, 1))
            prv = jnp.where(row == 0, rows(0, f), rollto(x, 1, 1))
            h = half_slope(nxt - x, x - prv)
            left.append(x + h)
            right.append(jnp.where(row == 7, rows(2, f), rollto(x - h, -1, 1)))
        fx = flux2(left, right, 0)
        for f in range(5):
            tx = fx[f] - jnp.where(row == 0, rows(3, f), rollto(fx[f], 1, 1))
            s = L[f, pl.ds(z0 + 2, PAIR)] + half * (tx + ty[f] + tz[f])
            adv[f, pl.ds(z0, PAIR)] = 0.5 * state[f, pl.ds(z0 + 4, PAIR)] + 0.5 * s
        return carry

    lax.fori_loop(0, 8 // PAIR, second_step, 0)
    adv_out[...] = adv[...]

    flat = adv[...].reshape(320, 128)
    y1 = jnp.dot(first[...], flat, precision=HIGHEST, preferred_element_type=F32)
    image = None
    col = 0
    lhs = []
    for k, chunk in enumerate(CHUNKS):
        n = len(chunk)
        y2 = jnp.concatenate([y1[(col + i) * 8 : (col + i) * 8 + 8] for i in range(n)], axis=1)
        v = jnp.dot(y2, second[col * 128 : (col + n) * 128, :], precision=HIGHEST, preferred_element_type=F32)
        col += n
        for f in range(5):
            lhs.append(dest[k * 5 + f] * v[f : f + 1, :])
    image = lax.dot_general(
        jnp.concatenate(lhs, axis=1), spots, (((1,), (1,)), ((), ())),
        precision=HIGHEST, preferred_element_type=F32,
    )
    sa[...] = image[:8]
    sb[...] = image[8:10]
    ga[0] = image[:8]
    gb[0] = image[8:10]
    ca = copies(sa, ga, y_peers, sem_as, sem_ar, 0)
    cb = copies(sb, gb, y_peers, sem_bs, sem_br, 0)
    for a, b in zip(ca, cb):
        a.start()
        b.start()

    nrow = ngy * 5
    q = iota((nrow, nlane), 0)
    lead = jnp.full((1, 1), agg[0], jnp.int32) == gy
    in_row = q - (starts >> 7)
    sel_a = jnp.where((in_row == iota((nrow, nlane), 1) % 8) & lead, 1.0, 0.0)
    q2 = iota((nrow, ngy * 2), 0)
    slot2 = iota((ngy, ngy * 2), 1) // 2
    before2 = jnp.where(turn(iota((ngy, ngy * 2), 0)) < turn(slot2), totals[:, : ngy * 2], 0.0)
    starts2 = jnp.sum(before2, axis=0, keepdims=True).astype(jnp.int32)
    sel_b = jnp.where((q2 - (starts2 >> 7) == 8 + iota((nrow, ngy * 2), 1) % 2) & lead, 1.0, 0.0)
    for a, b in zip(ca, cb):
        a.wait()
        b.wait()
    for k in range(ngy):
        gbrows[2 * k : 2 * k + 2, :] = gb[k]
    snap_out[...] = jnp.dot(
        sel_a, ga[...].reshape(ngy * 8, 128), precision=HIGHEST, preferred_element_type=F32
    ) + jnp.dot(sel_b, gbrows[...], precision=HIGHEST, preferred_element_type=F32)


def shards(ngx, ngy, state, counts, aggregator):
    nx = INNER[ngx]
    nz = ngx // nx
    first, second, ranks, cmat = tables()
    vm = pltpu.VMEM
    dma = pltpu.SemaphoreType.DMA
    nmax = ngy + nz + nx
    vmem = pl.BlockSpec(memory_space=pltpu.VMEM)
    adv, snap = pl.pallas_call(
        functools.partial(kernel, ngx, ngy),
        out_shape=(
            jax.ShapeDtypeStruct((5, 8, 8, 128), F32),
            jax.ShapeDtypeStruct((ngy * 5, 128), F32),
        ),
        in_specs=[vmem, vmem, pl.BlockSpec(memory_space=pltpu.SMEM)] + [vmem] * 4,
        out_specs=(vmem, vmem),
        scratch_shapes=[
            vm((5, 16, 8, 128), F32),
            vm((5, 12, 8, 128), F32),
            vm((5, 12, 8, 128), F32),
            vm((5, 12, 8, 128), F32),
            vm((5, 12, 8, 128), F32),
            vm((5, 12, 8, 128), F32),
            vm((5, 12, 8, 128), F32),
            vm((5, 8, 8, 128), F32),
            vm((5, 8, 8, 128), F32),
            vm((2, 5, 6, 8, 128), F32),
            vm((2, 5, 6, 8, 128), F32),
            vm((5, 8, 128), F32),
            vm((6, 5, 8, 128), F32),
            vm((2, 5, 2, 8, 128), F32),
            vm((3, 1, 128), F32),
            vm((ngy, 1, 128), F32),
            vm((nz, 1, 128), F32),
            vm((nx, 1, 128), F32),
            vm((ngy, 128), F32),
            vm((5, 8, 8, 128), F32),
            vm((ngy, 8, 128), F32),
            vm((ngy, 2, 128), F32),
            vm((8, 128), F32),
            vm((2, 128), F32),
            vm((ngy * 2, 128), F32),
            vm((2, 5, 7, 8, 128), F32),
            vm((4, 5, 8, 128), F32),
            dma((2,)), dma((2,)), dma((6,)), dma((6,)), dma((nmax,)), dma((nmax,)),
            dma((ngy,)), dma((ngy,)), dma((ngy,)), dma((ngy,)),
        ],
        compiler_params=pltpu.CompilerParams(collective_id=0, has_side_effects=True),
        name="step",
    )(state, counts, aggregator, first, second, ranks, cmat)
    return adv, snap.reshape(1, 1, ngy * 640)


def solution(mesh):
    ngx, ngy = mesh.shape["gx"], mesh.shape["gy"]
    placed = (P(None, None, "gx", "gy"), P(None, None, "gx", "gy"), P("gx"))
    return jax.shard_map(
        functools.partial(shards, ngx, ngy),
        mesh=mesh,
        in_specs=placed,
        out_specs=(P(None, None, "gx", "gy"), P("gx", "gy", None)),
        check_vma=False,
    )
```

time: 553 us -> 43.1 us (0.08)
  local copies, waits for them, and re-layouts: 243 us -> 2.22 us
  blocking collectives: 120 us -> 0 us
  waiting for transfers between devices: 115 us -> 0 us
  Pallas kernels: 0 us -> 39.4 us
  starting transfers between devices: 29.1 us -> 0 us
  other arithmetic: 21.2 us -> 0 us
  between operations: 17.7 us -> 1.29 us
  matrix products: 5.85 us -> 0 us
    scatter x2 -> x0, local copies, waits for them, and re-layouts: 211 us -> none  [the longest x1 150 us: shards(): stream = jnp.zeros((dev_cap,), jnp.float32).at[targets.reshape(-1)].set(v...]
    unnamed x2 -> x0, waiting for transfers between devices: 106 us -> none
    pmax x1 -> x0, blocking collectives: 95.9 us -> none  [step_size(): return COURANT / lax.pmax(local_top, ('gx', 'gy'))]
    pallas_call x0 -> x1, Pallas kernels: none -> 39.4 us  [shards(): pl.pallas_call(functools.partial(kernel, ngx, ngy), out_shape=(jax.ShapeD...]
    ppermute x8 -> x0, starting transfers between devices: 29.1 us -> none  [the longest x4 18.9 us: extended(): lax.ppermute(head, axis, [((i + 1) % count, i) for i in range(count)])]
    unnamed x1 -> x0, blocking collectives: 24.5 us -> none
    concatenate x8 -> x0, other arithmetic: 9.82 us -> none  [the longest x4 9.55 us: extended(): jnp.concatenate([lax.ppermute(tail, axis, [(i, (i + 1) % count) for i in...]
    ppermute x8 -> x0, waiting for transfers between devices: 8.87 us -> none  [the longest x4 4.92 us: extended(): lax.ppermute(tail, axis, [(i, (i + 1) % count) for i in range(count)])]
  transfers between devices with their start and end apart: 9 -> 0, of which waited for: 4 -> 0; matrix products, arithmetic and copies ran while one was open for 3% -> 0% of each run, Pallas kernels for 0% -> 0%
where the time goes in v1:
time: 43.1 us; the launch traced here: 42.9 us
  Pallas kernels  39.4 us (91%)
  local copies, waits for them, and re-layouts  2.22 us (5%)
  between operations  1.29 us (3%)
    pallas_call x1, Pallas kernels, shards(): pl.pallas_call(functools.partial(kernel, ngx, ngy), out_shape=(jax.ShapeD...  39.4 us
    unnamed x4, local copies, waits for them, and re-layouts  2.22 us

profile of v1, /device:TPU:1, one launch (start us, length us, event | category | flops | bytes accessed | tf_op | source)
XLA Modules:
  0.0 42.9 jit_solution(6957898314862831925)
XLA Ops:
  1.3 39.4 %step.1 = (f32[5,8,8,128]{3,2,1,0:T(8,128)}, f32[80,128]{1,0:T(8,128)}) custom-call(f32[5,16,8,128]{3,2,1,0:T(8,128)} %state.1, s32[5,1,1,16]{3,2,1,0:T(1,128)} %counts.1, s32[1]{0:T(128)S(6)} %copy.11.agg, f32[56,320]{1,0:T(8,128)} %constant.8.clone.first, f32[896,128]{1,0:T(8,128)} %constant.9.clone.second, s32[2,128]{1,0:T(2,128)} %constant.10.clone.ranks, ...), custom_call_target="tpu_custom_call" | custom-call | tf_op jit(solution)/shard_map/step/pallas_call | solution.py:565
  40.7 0.0 copy-start
  40.7 1.6 %copy.12 = f32[5,8,8,128]{3,2,1,0:T(8,128)} copy(f32[5,8,8,128]{3,2,1,0:T(8,128)} %get-tuple-element.8) | data formatting | bytes 327680
  42.3 0.0 copy-done
  42.3 0.6 %copy.13 = f32[1,1,10240]{2,1,0:T(1,128)} copy(f32[1,1,10240]{2,1,0:T(1,128)S(1)} %bitcast.1) | data formatting | bytes 81920
Async XLA Ops:
  40.7 1.6 %copy-start = (f32[80,128]{1,0:T(8,128)S(1)}, f32[80,128]{1,0:T(8,128)}, u32[]{:S(2)}) copy-start(f32[80,128]{1,0:T(8,128)} %get-tuple-element.5) | copy-start | bytes 122884

commit v2 on v1

--- a/solution.py
+++ b/solution.py
@@ -11,7 +11,7 @@
 
 MESH = pl.DeviceIdType.MESH
 F32 = jnp.float32
-HIGHEST = lax.Precision.HIGHEST
+BF16 = jnp.bfloat16
 GAMMA = 1.4
 COURANT = 0.1
 INNER = {32: 4, 4: 2}
@@ -59,7 +59,11 @@
     b = np.arange(16)[:, None]
     lane = np.arange(128)[None, :] % 16
     count = np.concatenate([(b < lane), (b == lane), np.ones((16, 128))], axis=1).astype(np.float32)
-    return first, second, ranks, count
+    first_hi = first.astype(BF16)
+    first_lo = (first - first_hi.astype(np.float32)).astype(BF16)
+    second_hi = second.astype(BF16)
+    second_lo = (second - second_hi.astype(np.float32)).astype(BF16)
+    return np.concatenate([first_hi, first_lo]), np.stack([second_hi, second_lo]), ranks, count
 
 
 def half_slope(a, b):
@@ -101,6 +105,15 @@
 
 def add(a, b):
     return [x + y for x, y in zip(a, b)]
+
+
+def split(x):
+    hi = x.astype(BF16)
+    return hi, (x - hi.astype(F32)).astype(BF16)
+
+
+def mm(a, b):
+    return jnp.dot(a, b, preferred_element_type=F32)
 
 
 def rollto(x, shift, axis):
@@ -204,25 +217,39 @@
 
 
 def kernel(
-    ngx, ngy, state, counts, agg, first, second, ranks, cmat,
-    adv_out, snap_out,
+    ngx, ngy, state_in, counts_in, agg_in, first_in, second_in, ranks_in, cmat_in,
+    adv, snap_out,
+    state, counts, agg, first, second, ranks, cmat, sem_in,
     W, XH, L, Lx, Wx, E1, E2, E1x, E2x, sendx, recvx, qown, recvq, qx,
-    maxsend, ry, rz, rx, tot, adv,
+    maxsend, ry, rz, rx, tot,
     ga, gb, sa, sb, gbrows, xedge, xinj,
     sem_hs, sem_hr, sem_qs, sem_qr, sem_ms, sem_mr, sem_as, sem_ar, sem_bs, sem_br,
 ):
+    loads = [
+        pltpu.make_async_copy(src, dst, sem_in.at[i])
+        for i, (src, dst) in enumerate(
+            [(state_in.at[:, 4:12], state.at[:, 4:12]), (counts_in, counts), (cmat_in, cmat)]
+            + [(state_in.at[:, 0:4], state.at[:, 0:4]), (state_in.at[:, 12:16], state.at[:, 12:16])]
+            + [(agg_in, agg), (ranks_in, ranks), (first_in, first), (second_in, second)]
+        )
+    ]
+    for c in loads:
+        c.start()
+
     nx = INNER[ngx]
     nz = ngx // nx
     gx = lax.axis_index("gx")
     gy = lax.axis_index("gy")
-    zc, xc = gx // nx, gx % nx
+    zc, xc = lax.div(gx, nx), lax.rem(gx, nx)
 
     def at(dx, dy):
-        return ((gx + dx + ngx) % ngx, (gy + dy + ngy) % ngy)
+        x = lax.rem(gx + (dx % ngx), ngx) if dx else gx
+        y = lax.rem(gy + (dy % ngy), ngy) if dy else gy
+        return (x, y)
 
     y_peers = [at(0, k) for k in range(1, ngy)]
-    z_peers = [(((zc + k) % nz) * nx + xc, gy) for k in range(1, nz)]
-    x_peers = [(zc * nx + (xc + k) % nx, gy) for k in range(1, nx)]
+    z_peers = [(lax.rem(zc + k, nz) * nx + xc, gy) for k in range(1, nz)]
+    x_peers = [(zc * nx + lax.rem(xc + k, nx), gy) for k in range(1, nx)]
     halo_peers = [at(-1, 0), at(1, 0)]
     q_peers = [at(-dx, -dy) for dx, dy in CORNERS]
 
@@ -231,15 +258,16 @@
     for peer in everyone:
         pl.semaphore_signal(barrier, inc=1, device_id=peer, device_id_type=MESH)
 
+    for c in loads[:3]:
+        c.wait()
     vmax = None
-    for z in range(16):
+    for z in range(4, 12):
         w = prims_of([state[f, z] for f in range(5)])
         for f in range(5):
             W[f, z] = w[f]
-        if 4 <= z < 12:
-            c = jnp.sqrt(GAMMA * w[4] / w[0])
-            s = jnp.maximum(jnp.maximum(jnp.abs(w[1]), jnp.abs(w[2])), jnp.abs(w[3])) + c
-            vmax = s if vmax is None else jnp.maximum(vmax, s)
+        c = jnp.sqrt(GAMMA * w[4] / w[0])
+        s = jnp.maximum(jnp.maximum(jnp.abs(w[1]), jnp.abs(w[2])), jnp.abs(w[3])) + c
+        vmax = s if vmax is None else jnp.maximum(vmax, s)
     top = jnp.max(jnp.max(vmax, axis=0, keepdims=True), axis=1, keepdims=True)
 
     cnt = jnp.zeros((8, 16), F32)
@@ -251,14 +279,6 @@
     lane1 = iota((1, 128), 1)
     maxsend[0] = jnp.where(lane1 < 64, top, total)
     ry[0] = maxsend[0]
-
-    row8 = iota((8, 128), 0)
-    for f in range(5):
-        for k in range(6):
-            lo, hi = state[f, 2 + k], state[f, 8 + k]
-            sendx[0, f, k] = jnp.where(row8 < 4, lo, rollto(hi, 4, 0))
-            sendx[1, f, k] = jnp.where(row8 < 4, rollto(lo, 4, 0), hi)
-        qown[f] = pack_columns(lambda z: state[f, z], range(16))
 
     pl.semaphore_wait(barrier, len(everyone))
 
@@ -274,6 +294,15 @@
     cy = copies(maxsend.at[0], ry, y_peers, sem_ms, sem_mr, 0)
     for c in cy:
         c.start()
+    for c in loads[3:]:
+        c.wait()
+    row8 = iota((8, 128), 0)
+    for f in range(5):
+        for k in range(6):
+            lo, hi = state[f, 2 + k], state[f, 8 + k]
+            sendx[0, f, k] = jnp.where(row8 < 4, lo, rollto(hi, 4, 0))
+            sendx[1, f, k] = jnp.where(row8 < 4, rollto(lo, 4, 0), hi)
+        qown[f] = pack_columns(lambda z: state[f, z], range(16))
     cq = [
         pltpu.make_async_remote_copy(
             src_ref=qown, dst_ref=recvq.at[i], send_sem=sem_qs.at[i], recv_sem=sem_qr.at[i],
@@ -292,6 +321,11 @@
     ]
     for c in ch:
         c.start()
+
+    for z in (*range(0, 4), *range(12, 16)):
+        w = prims_of([state[f, z] for f in range(5)])
+        for f in range(5):
+            W[f, z] = w[f]
 
     def load(ref, start, n):
         return [ref[f, pl.ds(start, n)] for f in range(5)]
@@ -438,7 +472,7 @@
         lane_to = pos & 127
         for f in range(5):
             dest.append(row_to[f : f + 1, :])
-            spots.append((iota((128, 128), 0) == lane_to[f : f + 1, :]).astype(F32))
+            spots.append((iota((128, 128), 0) == lane_to[f : f + 1, :]).astype(F32).astype(BF16))
     spots = jnp.concatenate(spots, axis=1)
     dest = [(iota((16, 128), 0) == d).astype(F32) for d in dest]
 
@@ -506,24 +540,29 @@
         return carry
 
     lax.fori_loop(0, 8 // PAIR, second_step, 0)
-    adv_out[...] = adv[...]
-
-    flat = adv[...].reshape(320, 128)
-    y1 = jnp.dot(first[...], flat, precision=HIGHEST, preferred_element_type=F32)
-    image = None
+
+    hi, lo = split(adv[...].reshape(320, 128))
+    y1 = mm(first[...], hi)
+    y1 = y1[:56] + y1[56:] + mm(first[:56, :], lo)
     col = 0
-    lhs = []
+    lhs_hi, lhs_lo = [], []
     for k, chunk in enumerate(CHUNKS):
         n = len(chunk)
         y2 = jnp.concatenate([y1[(col + i) * 8 : (col + i) * 8 + 8] for i in range(n)], axis=1)
-        v = jnp.dot(y2, second[col * 128 : (col + n) * 128, :], precision=HIGHEST, preferred_element_type=F32)
+        hi, lo = split(y2)
+        rows = slice(col * 128, (col + n) * 128)
+        v = mm(hi, second[0, rows, :]) + mm(lo, second[0, rows, :]) + mm(hi, second[1, rows, :])
         col += n
-        for f in range(5):
-            lhs.append(dest[k * 5 + f] * v[f : f + 1, :])
+        vh = v.astype(BF16).astype(F32)
+        vl = v - vh
+        for f in range(5):
+            lhs_hi.append(dest[k * 5 + f] * vh[f : f + 1, :])
+            lhs_lo.append(dest[k * 5 + f] * vl[f : f + 1, :])
+    lhs = jnp.concatenate([jnp.concatenate(lhs_hi, axis=1), jnp.concatenate(lhs_lo, axis=1)], axis=0)
     image = lax.dot_general(
-        jnp.concatenate(lhs, axis=1), spots, (((1,), (1,)), ((), ())),
-        precision=HIGHEST, preferred_element_type=F32,
+        lhs.astype(BF16), spots, (((1,), (1,)), ((), ())), preferred_element_type=F32
     )
+    image = image[:16] + image[16:]
     sa[...] = image[:8]
     sb[...] = image[8:10]
     ga[0] = image[:8]
@@ -549,9 +588,10 @@
         b.wait()
     for k in range(ngy):
         gbrows[2 * k : 2 * k + 2, :] = gb[k]
-    snap_out[...] = jnp.dot(
-        sel_a, ga[...].reshape(ngy * 8, 128), precision=HIGHEST, preferred_element_type=F32
-    ) + jnp.dot(sel_b, gbrows[...], precision=HIGHEST, preferred_element_type=F32)
+    sel_a, sel_b = sel_a.astype(BF16), sel_b.astype(BF16)
+    hi, lo = split(ga[...].reshape(ngy * 8, 128))
+    hi2, lo2 = split(gbrows[...])
+    snap_out[...] = (mm(sel_a, hi) + mm(sel_b, hi2)) + (mm(sel_a, lo) + mm(sel_b, lo2))
 
 
 def shards(ngx, ngy, state, counts, aggregator):
@@ -565,12 +605,20 @@
     adv, snap = pl.pallas_call(
         functools.partial(kernel, ngx, ngy),
         out_shape=(
-            jax.ShapeDtypeStruct((5, 8, 8, 128), F32),
-            jax.ShapeDtypeStruct((ngy * 5, 128), F32),
+            vm((5, 8, 8, 128), F32),
+            vm((ngy * 5, 128), F32),
         ),
-        in_specs=[vmem, vmem, pl.BlockSpec(memory_space=pltpu.SMEM)] + [vmem] * 4,
+        in_specs=[pl.BlockSpec(memory_space=pltpu.HBM)] * 7,
         out_specs=(vmem, vmem),
         scratch_shapes=[
+            vm(state.shape, F32),
+            vm(counts.shape, jnp.int32),
+            pltpu.SMEM((1,), jnp.int32),
+            vm(first.shape, BF16),
+            vm(second.shape, BF16),
+            vm(ranks.shape, jnp.int32),
+            vm(cmat.shape, F32),
+            dma((9,)),
             vm((5, 16, 8, 128), F32),
             vm((5, 12, 8, 128), F32),
             vm((5, 12, 8, 128), F32),
@@ -590,7 +638,6 @@
             vm((nz, 1, 128), F32),
             vm((nx, 1, 128), F32),
             vm((ngy, 128), F32),
-            vm((5, 8, 8, 128), F32),
             vm((ngy, 8, 128), F32),
             vm((ngy, 2, 128), F32),
             vm((8, 128), F32),

time: 43.1 us -> 39.5 us (0.916)
  Pallas kernels: 39.4 us -> 36.8 us
  local copies, waits for them, and re-layouts: 2.22 us -> 1.29 us
    pallas_call x1, Pallas kernels: 39.4 us -> 36.8 us  [shards(): pl.pallas_call(functools.partial(kernel, ngx, ngy), out_shape=(vm((5, 8,...]
    unnamed x4 -> x2, local copies, waits for them, and re-layouts: 2.22 us -> 1.29 us
where the time goes in v2:
time: 39.5 us; the launch traced here: 39.4 us
  Pallas kernels  36.8 us (93%)
  local copies, waits for them, and re-layouts  1.29 us (3%)
  between operations  1.28 us (3%)
    pallas_call x1, Pallas kernels, shards(): pl.pallas_call(functools.partial(kernel, ngx, ngy), out_shape=(vm((5, 8,...  36.8 us
    unnamed x2, local copies, waits for them, and re-layouts  1.29 us

profile of v2, /device:TPU:1, one launch (start us, length us, event | category | flops | bytes accessed | tf_op | source)
XLA Modules:
  0.0 39.4 jit_solution(4333600758633527845)
XLA Ops:
  1.3 36.8 %step.1 = (f32[5,8,8,128]{3,2,1,0:T(8,128)S(1)}, f32[80,128]{1,0:T(8,128)S(1)}) custom-call(f32[5,16,8,128]{3,2,1,0:T(8,128)} %state_in.1, s32[5,1,1,16]{3,2,1,0:T(1,128)} %counts_in.1, s32[1]{0:T(128)S(6)} %copy.13.agg_in, bf16[112,320]{1,0:T(8,128)(2,1)} %constant.8.clone.first_in, bf16[2,896,128]{2,1,0:T(8,128)(2,1)} %constant.9.clone.second_in, ...), custom_call_target="tpu_custom_call" | custom-call | tf_op jit(solution)/shard_map/step/pallas_call | solution.py:605
  38.1 0.7 %copy.11 = f32[5,8,8,128]{3,2,1,0:T(8,128)} copy(f32[5,8,8,128]{3,2,1,0:T(8,128)S(1)} %get-tuple-element.6) | data formatting | bytes 327680
  38.7 0.6 %copy.12 = f32[1,1,10240]{2,1,0:T(1,128)} copy(f32[1,1,10240]{2,1,0:T(1,128)S(1)} %bitcast.1) | data formatting | bytes 81920

commit v3 on v2

--- a/solution.py
+++ b/solution.py
@@ -14,7 +14,6 @@
 BF16 = jnp.bfloat16
 GAMMA = 1.4
 COURANT = 0.1
-INNER = {32: 4, 4: 2}
 PAIR = 2
 CORNERS = [(0, -1), (0, 1), (1, -1), (-1, -1), (1, 1), (-1, 1)]
 CHUNKS = [[((0, 0), 4), ((0, 1), 3), ((0, 3), 1)], [((0, 2), 2), ((1, 0), 3), ((1, 1), 1), ((2, 0), 1)]]
@@ -67,7 +66,7 @@
 
 
 def half_slope(a, b):
-    return 0.5 * (jnp.maximum(jnp.minimum(a, b), 0.0) + jnp.minimum(jnp.maximum(a, b), 0.0))
+    return 0.5 * jnp.maximum(jnp.minimum(a, jnp.maximum(b, 0.0)), jnp.minimum(b, 0.0))
 
 
 def prims_of(cons):
@@ -78,33 +77,27 @@
     return [rho, u, v, w, p]
 
 
-def side_terms(q, comp):
-    rho, p = q[0], q[4]
-    vel = q[1:4]
-    vn = vel[comp]
-    mom = [rho * x for x in vel]
-    en = p * (1.0 / (GAMMA - 1.0)) + 0.5 * (mom[0] * vel[0] + mom[1] * vel[1] + mom[2] * vel[2])
-    rows = [mom[comp]]
-    for i in range(3):
-        t = mom[i] * vn
-        rows.append(t + p if i == comp else t)
-    rows.append((en + p) * vn)
-    return [rho] + mom + [en], rows, jnp.abs(vn) + jnp.sqrt(GAMMA * p / rho)
+def root(x):
+    return x * lax.rsqrt(jnp.maximum(x, 1e-37))
 
 
 def flux2(left, right, comp):
-    ul, fl, sl = side_terms(left, comp)
-    ur, fr, sr = side_terms(right, comp)
-    a = jnp.maximum(sl, sr)
-    return [(x + y) - a * (d - c) for x, y, c, d in zip(fl, fr, ul, ur)]
-
-
-def sub(a, b):
-    return [x - y for x, y in zip(a, b)]
-
-
-def add(a, b):
-    return [x + y for x, y in zip(a, b)]
+    a = None
+    for q in (left, right):
+        s = jnp.abs(q[1 + comp]) + root(GAMMA * q[4] / q[0])
+        a = s if a is None else jnp.maximum(a, s)
+    out = None
+    for q, away in ((left, None), (right, a)):
+        rho, p, vel = q[0], q[4], q[1:4]
+        vn = vel[comp]
+        shift = vn + a if away is None else vn - a
+        mass = rho * shift
+        kin = 0.5 * (vel[0] * vel[0] + vel[1] * vel[1] + vel[2] * vel[2])
+        rows = [mass] + [mass * v for v in vel]
+        rows[1 + comp] = rows[1 + comp] + p
+        rows.append(mass * kin + p * (shift * (1.0 / (GAMMA - 1.0)) + vn))
+        out = rows if out is None else [x + y for x, y in zip(out, rows)]
+    return out
 
 
 def split(x):
@@ -221,9 +214,9 @@
     adv, snap_out,
     state, counts, agg, first, second, ranks, cmat, sem_in,
     W, XH, L, Lx, Wx, E1, E2, E1x, E2x, sendx, recvx, qown, recvq, qx,
-    maxsend, ry, rz, rx, tot,
-    ga, gb, sa, sb, gbrows, xedge, xinj,
-    sem_hs, sem_hr, sem_qs, sem_qr, sem_ms, sem_mr, sem_as, sem_ar, sem_bs, sem_br,
+    maxsend, ry, rw, tot,
+    ga, sa, xedge, xinj, pick,
+    sem_h, sem_q, sem_y, sem_w, sem_a,
 ):
     loads = [
         pltpu.make_async_copy(src, dst, sem_in.at[i])
@@ -236,11 +229,8 @@
     for c in loads:
         c.start()
 
-    nx = INNER[ngx]
-    nz = ngx // nx
     gx = lax.axis_index("gx")
     gy = lax.axis_index("gy")
-    zc, xc = lax.div(gx, nx), lax.rem(gx, nx)
 
     def at(dx, dy):
         x = lax.rem(gx + (dx % ngx), ngx) if dx else gx
@@ -248,13 +238,14 @@
         return (x, y)
 
     y_peers = [at(0, k) for k in range(1, ngy)]
-    z_peers = [(lax.rem(zc + k, nz) * nx + xc, gy) for k in range(1, nz)]
-    x_peers = [(zc * nx + lax.rem(xc + k, nx), gy) for k in range(1, nx)]
+    w_peers = [at(k, 0) for k in range(1, ngx)]
     halo_peers = [at(-1, 0), at(1, 0)]
     q_peers = [at(-dx, -dy) for dx, dy in CORNERS]
 
     barrier = pltpu.get_barrier_semaphore()
-    everyone = y_peers + z_peers + x_peers + halo_peers + q_peers[2:]
+    far_w = sorted(range(1, ngx), key=lambda k: abs(k - ngx // 2))
+    far_y = sorted(range(1, ngy), key=lambda k: abs(k - ngy // 2))
+    everyone = [w_peers[k - 1] for k in far_w] + [y_peers[k - 1] for k in far_y] + q_peers[2:]
     for peer in everyone:
         pl.semaphore_signal(barrier, inc=1, device_id=peer, device_id_type=MESH)
 
@@ -265,7 +256,7 @@
         w = prims_of([state[f, z] for f in range(5)])
         for f in range(5):
             W[f, z] = w[f]
-        c = jnp.sqrt(GAMMA * w[4] / w[0])
+        c = root(GAMMA * w[4] / w[0])
         s = jnp.maximum(jnp.maximum(jnp.abs(w[1]), jnp.abs(w[2])), jnp.abs(w[3])) + c
         vmax = s if vmax is None else jnp.maximum(vmax, s)
     top = jnp.max(jnp.max(vmax, axis=0, keepdims=True), axis=1, keepdims=True)
@@ -282,18 +273,25 @@
 
     pl.semaphore_wait(barrier, len(everyone))
 
-    def copies(src, bufs, peers, send, recv, base):
-        return [
+    def send(src, bufs, peers, order, sems):
+        for k in order:
             pltpu.make_async_remote_copy(
-                src_ref=src, dst_ref=bufs.at[k + 1], send_sem=send.at[base + k], recv_sem=recv.at[base + k],
-                device_id=peer, device_id_type=MESH,
-            )
-            for k, peer in enumerate(peers)
-        ]
-
-    cy = copies(maxsend.at[0], ry, y_peers, sem_ms, sem_mr, 0)
-    for c in cy:
-        c.start()
+                src_ref=src, dst_ref=bufs.at[k], send_sem=sems.at[0], recv_sem=sems.at[1],
+                device_id=peers[k], device_id_type=MESH,
+            ).start()
+
+    def whole(ref, sems):
+        return pltpu.make_async_remote_copy(
+            src_ref=ref, dst_ref=ref, send_sem=sems.at[0], recv_sem=sems.at[1],
+            device_id=y_peers[0], device_id_type=MESH,
+        )
+
+    y_of = dict(zip(range(1, ngy), y_peers))
+    w_of = dict(zip(range(1, ngx), w_peers))
+    all_y, all_w = whole(ry.at[pl.ds(1, ngy - 1)], sem_y), whole(rw.at[pl.ds(1, ngx - 1)], sem_w)
+    all_q, all_h = whole(recvq, sem_q), whole(recvx, sem_h)
+    all_a = whole(ga.at[pl.ds(1, ngy - 1), pl.ds(0, 10)], sem_a)
+    send(maxsend.at[0], ry, y_of, far_y, sem_y)
     for c in loads[3:]:
         c.wait()
     row8 = iota((8, 128), 0)
@@ -303,25 +301,12 @@
             sendx[0, f, k] = jnp.where(row8 < 4, lo, rollto(hi, 4, 0))
             sendx[1, f, k] = jnp.where(row8 < 4, rollto(lo, 4, 0), hi)
         qown[f] = pack_columns(lambda z: state[f, z], range(16))
-    cq = [
+    send(qown, recvq, q_peers, range(6), sem_q)
+    for i, peer in enumerate(halo_peers):
         pltpu.make_async_remote_copy(
-            src_ref=qown, dst_ref=recvq.at[i], send_sem=sem_qs.at[i], recv_sem=sem_qr.at[i],
+            src_ref=sendx.at[i], dst_ref=recvx.at[i], send_sem=sem_h.at[0], recv_sem=sem_h.at[1],
             device_id=peer, device_id_type=MESH,
-        )
-        for i, peer in enumerate(q_peers)
-    ]
-    for c in cq:
-        c.start()
-    ch = [
-        pltpu.make_async_remote_copy(
-            src_ref=sendx.at[i], dst_ref=recvx.at[i], send_sem=sem_hs.at[i], recv_sem=sem_hr.at[i],
-            device_id=peer, device_id_type=MESH,
-        )
-        for i, peer in enumerate(halo_peers)
-    ]
-    for c in ch:
-        c.start()
-
+        ).start()
     for z in (*range(0, 4), *range(12, 16)):
         w = prims_of([state[f, z] for f in range(5)])
         for f in range(5):
@@ -339,22 +324,17 @@
 
     lax.fori_loop(0, 12 // PAIR, z_main, 0)
 
-    for c in cy:
-        c.wait()
+    all_y.wait_recv()
     best = ry[0]
     for k in range(ngy):
         if k:
             best = jnp.maximum(best, ry[k])
         tot[k : k + 1, :] = jnp.where(lane1 < 64, rollto(ry[k], 64, 1), ry[k])
     maxsend[1] = jnp.where(lane1 < 64, best, rollto(best, 64, 1))
-    cz = copies(maxsend.at[1], rz, z_peers, sem_ms, sem_mr, ngy)
-    for c in cz:
-        c.start()
-
-    for c in cq:
-        c.wait()
-    for c in ch:
-        c.wait()
+    send(maxsend.at[1], rw, w_of, far_w, sem_w)
+
+    all_q.wait_recv()
+    all_h.wait_recv()
     for f in range(5):
         for k in range(6):
             a, b = recvx[0, f, k], recvx[1, f, k]
@@ -413,16 +393,6 @@
 
     lax.fori_loop(0, 12 // PAIR, xy_main, 0)
 
-    for c in cz:
-        c.wait()
-    best = maxsend[1]
-    for k in range(1, nz):
-        best = jnp.maximum(best, rz[k])
-    maxsend[2] = best
-    cx = copies(maxsend.at[2], rx, x_peers, sem_ms, sem_mr, ngy + nz)
-    for c in cx:
-        c.start()
-
     def strip(i, carry):
         z0 = i * PAIR
         w = load(Wx, z0, PAIR + 4)
@@ -443,16 +413,18 @@
                 xedge[0, f, j + 4, z : z + 1, :] = state[f, z + 4, r : r + 1, :]
                 xedge[1, f, j + 4, z : z + 1, :] = L[f, z + 2, r : r + 1, :]
 
-    me_rank = jnp.full((1, 1), (gy - agg[0] + ngy) % ngy, jnp.int32)
-    nlane = ngy * 8
+    leader = agg[...]
+    me_rank = (gy - leader + ngy) & (ngy - 1)
+    nlane = ngy * 16
     slot_col = iota((ngy, nlane), 0)
-    slot_row = iota((ngy, nlane), 1) // 8
+    slot_row = iota((ngy, nlane), 1) // 16
 
     def turn(slot):
-        return (gy - slot - agg[0] + 2 * ngy) & (ngy - 1)
+        return (gy - slot - leader + 2 * ngy) & (ngy - 1)
 
     totals = tot[...]
-    before = jnp.where(turn(slot_col) < turn(slot_row), totals[:, :nlane], 0.0)
+    wide = jnp.broadcast_to(totals[:, :1], (ngy, nlane))
+    before = jnp.where(turn(slot_col) < turn(slot_row), wide, 0.0)
     starts = jnp.sum(before, axis=0, keepdims=True).astype(jnp.int32)
     mine = jnp.sum(
         jnp.where(turn(iota((ngy, 128), 0)) < me_rank, totals, 0.0), axis=0, keepdims=True
@@ -476,11 +448,17 @@
     spots = jnp.concatenate(spots, axis=1)
     dest = [(iota((16, 128), 0) == d).astype(F32) for d in dest]
 
-    for c in cx:
-        c.wait()
-    best = maxsend[2]
-    for k in range(1, nx):
-        best = jnp.maximum(best, rx[k])
+    nrow = ngy * 5
+    q = iota((nrow, nlane), 0)
+    lead = me_rank == 0
+    in_row = q - (starts >> 7)
+    pick[...] = jnp.where((in_row == iota((nrow, nlane), 1) % 16) & lead, 1.0, 0.0).astype(BF16)
+    ga[:, 10:16] = jnp.zeros((ngy, 6, 128), F32)
+
+    all_w.wait_recv()
+    best = maxsend[1]
+    for k in range(1, ngx):
+        best = jnp.maximum(best, rw[k])
     ratio = COURANT / best
     half = -0.5 * ratio
 
@@ -502,25 +480,20 @@
     for f in range(5):
         xinj[3, f] = fx[f]
 
-    def section(i, carry):
-        z0 = i * PAIR
-        s = [state[f, pl.ds(z0 + 2, PAIR)] + half * L[f, pl.ds(z0, PAIR)] for f in range(5)]
+    for z in range(12):
+        s = [state[f, z + 2] + half * L[f, z] for f in range(5)]
         w = prims_of(s)
         for f in range(5):
-            L[f, pl.ds(z0, PAIR)] = s[f]
-            W[f, pl.ds(z0, PAIR)] = w[f]
-        return carry
-
-    lax.fori_loop(0, 12 // PAIR, section, 0)
-
-    def second_step(i, carry):
-        z0 = i * PAIR
+            L[f, z] = s[f]
+            W[f, z] = w[f]
+
+    for z0 in range(0, 8, PAIR):
         w = load(W, z0, PAIR + 4)
         tz = z_term(w)
         c = [x[2:-2] for x in w]
         ty = y_term(c, load(E1, z0, PAIR), load(E2, z0, PAIR))
 
-        def rows(j, f):
+        def rows(j, f, z0=z0):
             return jnp.stack([xinj[j, f, pl.ds(z0 + d, 1), :] for d in range(PAIR)])
 
         row = iota(c[0].shape, 1)
@@ -537,9 +510,7 @@
             tx = fx[f] - jnp.where(row == 0, rows(3, f), rollto(fx[f], 1, 1))
             s = L[f, pl.ds(z0 + 2, PAIR)] + half * (tx + ty[f] + tz[f])
             adv[f, pl.ds(z0, PAIR)] = 0.5 * state[f, pl.ds(z0 + 4, PAIR)] + 0.5 * s
-        return carry
-
-    lax.fori_loop(0, 8 // PAIR, second_step, 0)
+
 
     hi, lo = split(adv[...].reshape(320, 128))
     y1 = mm(first[...], hi)
@@ -563,44 +534,21 @@
         lhs.astype(BF16), spots, (((1,), (1,)), ((), ())), preferred_element_type=F32
     )
     image = image[:16] + image[16:]
-    sa[...] = image[:8]
-    sb[...] = image[8:10]
-    ga[0] = image[:8]
-    gb[0] = image[8:10]
-    ca = copies(sa, ga, y_peers, sem_as, sem_ar, 0)
-    cb = copies(sb, gb, y_peers, sem_bs, sem_br, 0)
-    for a, b in zip(ca, cb):
-        a.start()
-        b.start()
-
-    nrow = ngy * 5
-    q = iota((nrow, nlane), 0)
-    lead = jnp.full((1, 1), agg[0], jnp.int32) == gy
-    in_row = q - (starts >> 7)
-    sel_a = jnp.where((in_row == iota((nrow, nlane), 1) % 8) & lead, 1.0, 0.0)
-    q2 = iota((nrow, ngy * 2), 0)
-    slot2 = iota((ngy, ngy * 2), 1) // 2
-    before2 = jnp.where(turn(iota((ngy, ngy * 2), 0)) < turn(slot2), totals[:, : ngy * 2], 0.0)
-    starts2 = jnp.sum(before2, axis=0, keepdims=True).astype(jnp.int32)
-    sel_b = jnp.where((q2 - (starts2 >> 7) == 8 + iota((nrow, ngy * 2), 1) % 2) & lead, 1.0, 0.0)
-    for a, b in zip(ca, cb):
-        a.wait()
-        b.wait()
-    for k in range(ngy):
-        gbrows[2 * k : 2 * k + 2, :] = gb[k]
-    sel_a, sel_b = sel_a.astype(BF16), sel_b.astype(BF16)
-    hi, lo = split(ga[...].reshape(ngy * 8, 128))
-    hi2, lo2 = split(gbrows[...])
-    snap_out[...] = (mm(sel_a, hi) + mm(sel_b, hi2)) + (mm(sel_a, lo) + mm(sel_b, lo2))
+    sa[...] = image
+    ga[0] = image
+    send(sa.at[pl.ds(0, 10)], ga.at[:, pl.ds(0, 10)], y_of, far_y, sem_a)
+
+    for c in (all_y, all_w, all_q, all_h):
+        c.wait_send()
+    all_a.wait()
+    hi, lo = split(ga[...].reshape(ngy * 16, 128))
+    snap_out[...] = mm(pick[...], hi) + mm(pick[...], lo)
 
 
 def shards(ngx, ngy, state, counts, aggregator):
-    nx = INNER[ngx]
-    nz = ngx // nx
     first, second, ranks, cmat = tables()
     vm = pltpu.VMEM
     dma = pltpu.SemaphoreType.DMA
-    nmax = ngy + nz + nx
     vmem = pl.BlockSpec(memory_space=pltpu.VMEM)
     adv, snap = pl.pallas_call(
         functools.partial(kernel, ngx, ngy),
@@ -613,7 +561,7 @@
         scratch_shapes=[
             vm(state.shape, F32),
             vm(counts.shape, jnp.int32),
-            pltpu.SMEM((1,), jnp.int32),
+            vm((1, 1), jnp.int32),
             vm(first.shape, BF16),
             vm(second.shape, BF16),
             vm(ranks.shape, jnp.int32),
@@ -633,24 +581,20 @@
             vm((5, 8, 128), F32),
             vm((6, 5, 8, 128), F32),
             vm((2, 5, 2, 8, 128), F32),
-            vm((3, 1, 128), F32),
+            vm((2, 1, 128), F32),
             vm((ngy, 1, 128), F32),
-            vm((nz, 1, 128), F32),
-            vm((nx, 1, 128), F32),
+            vm((ngx, 1, 128), F32),
             vm((ngy, 128), F32),
-            vm((ngy, 8, 128), F32),
-            vm((ngy, 2, 128), F32),
-            vm((8, 128), F32),
-            vm((2, 128), F32),
-            vm((ngy * 2, 128), F32),
+            vm((ngy, 16, 128), F32),
+            vm((16, 128), F32),
             vm((2, 5, 7, 8, 128), F32),
             vm((4, 5, 8, 128), F32),
-            dma((2,)), dma((2,)), dma((6,)), dma((6,)), dma((nmax,)), dma((nmax,)),
-            dma((ngy,)), dma((ngy,)), dma((ngy,)), dma((ngy,)),
+            vm((ngy * 5, ngy * 16), BF16),
+            dma((2,)), dma((2,)), dma((2,)), dma((2,)), dma((2,)),
         ],
         compiler_params=pltpu.CompilerParams(collective_id=0, has_side_effects=True),
         name="step",
-    )(state, counts, aggregator, first, second, ranks, cmat)
+    )(state, counts, aggregator.reshape(1, 1), first, second, ranks, cmat)
     return adv, snap.reshape(1, 1, ngy * 640)
 
 

time: 39.5 us -> 35.9 us (0.909)
  Pallas kernels: 36.8 us -> 33.2 us
    pallas_call x1, Pallas kernels: 36.8 us -> 33.2 us  [shards(): pl.pallas_call(functools.partial(kernel, ngx, ngy), out_shape=(vm((5, 8,...]
where the time goes in v3:
time: 35.9 us; the launch traced here: 35.8 us
  Pallas kernels  33.2 us (92%)
  local copies, waits for them, and re-layouts  1.29 us (4%)
  between operations  1.28 us (4%)
    pallas_call x1, Pallas kernels, shards(): pl.pallas_call(functools.partial(kernel, ngx, ngy), out_shape=(vm((5, 8,...  33.2 us
    unnamed x2, local copies, waits for them, and re-layouts  1.29 us

profile of v3, /device:TPU:1, one launch (start us, length us, event | category | flops | bytes accessed | tf_op | source)
XLA Modules:
  0.0 35.8 jit_solution(17637927006328322134)
XLA Ops:
  1.3 33.2 %step.1 = (f32[5,8,8,128]{3,2,1,0:T(8,128)S(1)}, f32[80,128]{1,0:T(8,128)S(1)}) custom-call(f32[5,16,8,128]{3,2,1,0:T(8,128)} %state_in.1, s32[5,1,1,16]{3,2,1,0:T(1,128)} %counts_in.1, s32[1,1]{1,0:T(1,128)} %bitcast.2.agg_in, bf16[112,320]{1,0:T(8,128)(2,1)} %constant.8.clone.first_in, bf16[2,896,128]{2,1,0:T(8,128)(2,1)} %constant.9.clone.second_in, ...), custom_call_target="tpu_custom_call" | custom-call | tf_op jit(solution)/shard_map/step/pallas_call | solution.py:553
  34.5 0.7 %copy.11 = f32[5,8,8,128]{3,2,1,0:T(8,128)} copy(f32[5,8,8,128]{3,2,1,0:T(8,128)S(1)} %get-tuple-element.6) | data formatting | bytes 327680
  35.2 0.6 %copy.12 = f32[1,1,10240]{2,1,0:T(1,128)} copy(f32[1,1,10240]{2,1,0:T(1,128)S(1)} %bitcast.3) | data formatting | bytes 81920

commit v4 on v3

--- a/solution.py
+++ b/solution.py
@@ -211,11 +211,11 @@
 
 def kernel(
     ngx, ngy, state_in, counts_in, agg_in, first_in, second_in, ranks_in, cmat_in,
-    adv, snap_out,
+    adv, ga, pick,
     state, counts, agg, first, second, ranks, cmat, sem_in,
     W, XH, L, Lx, Wx, E1, E2, E1x, E2x, sendx, recvx, qown, recvq, qx,
     maxsend, ry, rw, tot,
-    ga, sa, xedge, xinj, pick,
+    sa, xedge, xinj,
     sem_h, sem_q, sem_y, sem_w, sem_a,
 ):
     loads = [
@@ -541,8 +541,16 @@
     for c in (all_y, all_w, all_q, all_h):
         c.wait_send()
     all_a.wait()
-    hi, lo = split(ga[...].reshape(ngy * 16, 128))
-    snap_out[...] = mm(pick[...], hi) + mm(pick[...], lo)
+
+def place(adv, ga, pick, adv_out, snap_out, snap, sems):
+    first = pltpu.make_async_copy(adv, adv_out, sems.at[0])
+    first.start()
+    hi, lo = split(ga[...].reshape(ga.shape[0] * 16, 128))
+    snap[...] = mm(pick[...], hi) + mm(pick[...], lo)
+    second = pltpu.make_async_copy(snap, snap_out, sems.at[1])
+    second.start()
+    first.wait()
+    second.wait()
 
 
 def shards(ngx, ngy, state, counts, aggregator):
@@ -550,14 +558,15 @@
     vm = pltpu.VMEM
     dma = pltpu.SemaphoreType.DMA
     vmem = pl.BlockSpec(memory_space=pltpu.VMEM)
-    adv, snap = pl.pallas_call(
+    adv, images, pick = pl.pallas_call(
         functools.partial(kernel, ngx, ngy),
         out_shape=(
             vm((5, 8, 8, 128), F32),
-            vm((ngy * 5, 128), F32),
+            vm((ngy, 16, 128), F32),
+            vm((ngy * 5, ngy * 16), BF16),
         ),
         in_specs=[pl.BlockSpec(memory_space=pltpu.HBM)] * 7,
-        out_specs=(vmem, vmem),
+        out_specs=(vmem, vmem, vmem),
         scratch_shapes=[
             vm(state.shape, F32),
             vm(counts.shape, jnp.int32),
@@ -585,16 +594,24 @@
             vm((ngy, 1, 128), F32),
             vm((ngx, 1, 128), F32),
             vm((ngy, 128), F32),
-            vm((ngy, 16, 128), F32),
             vm((16, 128), F32),
             vm((2, 5, 7, 8, 128), F32),
             vm((4, 5, 8, 128), F32),
-            vm((ngy * 5, ngy * 16), BF16),
             dma((2,)), dma((2,)), dma((2,)), dma((2,)), dma((2,)),
         ],
         compiler_params=pltpu.CompilerParams(collective_id=0, has_side_effects=True),
         name="step",
     )(state, counts, aggregator.reshape(1, 1), first, second, ranks, cmat)
+    hbm = pl.BlockSpec(memory_space=pltpu.HBM)
+    adv, snap = pl.pallas_call(
+        place,
+        out_shape=(jax.ShapeDtypeStruct(adv.shape, F32), jax.ShapeDtypeStruct((ngy * 5, 128), F32)),
+        in_specs=[vmem] * 3,
+        out_specs=(hbm, hbm),
+        scratch_shapes=[vm((ngy * 5, 128), F32), dma((2,))],
+        compiler_params=pltpu.CompilerParams(vmem_limit_bytes=1 << 20),
+        name="place",
+    )(adv, images, pick)
     return adv, snap.reshape(1, 1, ngy * 640)
 
 

time: 35.9 us -> 35.3 us (0.983)
  local copies, waits for them, and re-layouts: 1.29 us -> 0 us
  Pallas kernels: 33.2 us -> 33.8 us
    unnamed x2 -> x0, local copies, waits for them, and re-layouts: 1.29 us -> none
    pallas_call x0 -> x1, Pallas kernels: none -> 0.8 us  [shards(): pl.pallas_call(place, out_shape=(jax.ShapeDtypeStruct(adv.shape, F32), ja...]
where the time goes in v4:
time: 35.3 us; the launch traced here: 35.1 us
  Pallas kernels  33.8 us (96%)
  between operations  1.28 us (4%)
    pallas_call x1, Pallas kernels, shards(): pl.pallas_call(functools.partial(kernel, ngx, ngy), out_shape=(vm((5, 8,...  33 us
    pallas_call x1, Pallas kernels, shards(): pl.pallas_call(place, out_shape=(jax.ShapeDtypeStruct(adv.shape, F32), ja...  0.8 us

profile of v4, /device:TPU:1, one launch (start us, length us, event | category | flops | bytes accessed | tf_op | source)
XLA Modules:
  0.0 35.1 jit_solution(16159584908233397950)
XLA Ops:
  1.3 33.0 %step.1 = (f32[5,8,8,128]{3,2,1,0:T(8,128)S(1)}, f32[16,16,128]{2,1,0:T(8,128)S(1)}, bf16[80,256]{1,0:T(8,128)(2,1)S(1)}) custom-call(f32[5,16,8,128]{3,2,1,0:T(8,128)} %state_in.1, s32[5,1,1,16]{3,2,1,0:T(1,128)} %counts_in.1, s32[1,1]{1,0:T(1,128)} %bitcast.2.agg_in, bf16[112,320]{1,0:T(8,128)(2,1)} %constant.8.clone.first_in, ...), custom_call_target="tpu_custom_call" | custom-call | tf_op jit(solution)/shard_map/step/pallas_call | solution.py:561
  34.3 0.8 %place.1 = (f32[5,8,8,128]{3,2,1,0:T(8,128)}, f32[80,128]{1,0:T(8,128)}) custom-call(f32[5,8,8,128]{3,2,1,0:T(8,128)S(1)} %get-tuple-element.7.adv, f32[16,16,128]{2,1,0:T(8,128)S(1)} %get-tuple-element.8.ga, bf16[80,256]{1,0:T(8,128)(2,1)S(1)} %get-tuple-element.9.pick), custom_call_target="tpu_custom_call" | custom-call | tf_op jit(solution)/shard_map/place/pallas_call | solution.py:606

commit v5 on v4

--- a/solution.py
+++ b/solution.py
@@ -245,7 +245,7 @@
     barrier = pltpu.get_barrier_semaphore()
     far_w = sorted(range(1, ngx), key=lambda k: abs(k - ngx // 2))
     far_y = sorted(range(1, ngy), key=lambda k: abs(k - ngy // 2))
-    everyone = [w_peers[k - 1] for k in far_w] + [y_peers[k - 1] for k in far_y] + q_peers[2:]
+    everyone = [y_peers[k - 1] for k in far_y] + [w_peers[k - 1] for k in far_w] + q_peers[2:]
     for peer in everyone:
         pl.semaphore_signal(barrier, inc=1, device_id=peer, device_id_type=MESH)
 
@@ -487,14 +487,14 @@
             L[f, z] = s[f]
             W[f, z] = w[f]
 
-    for z0 in range(0, 8, PAIR):
-        w = load(W, z0, PAIR + 4)
+    for z0 in range(0, 8, 4):
+        w = load(W, z0, 4 + 4)
         tz = z_term(w)
         c = [x[2:-2] for x in w]
-        ty = y_term(c, load(E1, z0, PAIR), load(E2, z0, PAIR))
+        ty = y_term(c, load(E1, z0, 4), load(E2, z0, 4))
 
         def rows(j, f, z0=z0):
-            return jnp.stack([xinj[j, f, pl.ds(z0 + d, 1), :] for d in range(PAIR)])
+            return jnp.stack([xinj[j, f, pl.ds(z0 + d, 1), :] for d in range(4)])
 
         row = iota(c[0].shape, 1)
         left, right, inj = [], [], []
@@ -508,8 +508,8 @@
         fx = flux2(left, right, 0)
         for f in range(5):
             tx = fx[f] - jnp.where(row == 0, rows(3, f), rollto(fx[f], 1, 1))
-            s = L[f, pl.ds(z0 + 2, PAIR)] + half * (tx + ty[f] + tz[f])
-            adv[f, pl.ds(z0, PAIR)] = 0.5 * state[f, pl.ds(z0 + 4, PAIR)] + 0.5 * s
+            s = L[f, pl.ds(z0 + 2, 4)] + half * (tx + ty[f] + tz[f])
+            adv[f, pl.ds(z0, 4)] = 0.5 * state[f, pl.ds(z0 + 4, 4)] + 0.5 * s
 
 
     hi, lo = split(adv[...].reshape(320, 128))

time: 35.3 us -> 34.9 us (0.989)
  no operation moved by 1% of the time
where the time goes in v5:
time: 34.9 us; the launch traced here: 34.8 us
  Pallas kernels  33.5 us (96%)
  between operations  1.28 us (4%)
    pallas_call x1, Pallas kernels, shards(): pl.pallas_call(functools.partial(kernel, ngx, ngy), out_shape=(vm((5, 8,...  32.7 us
    pallas_call x1, Pallas kernels, shards(): pl.pallas_call(place, out_shape=(jax.ShapeDtypeStruct(adv.shape, F32), ja...  0.8 us

profile of v5, /device:TPU:1, one launch (start us, length us, event | category | flops | bytes accessed | tf_op | source)
XLA Modules:
  0.0 34.8 jit_solution(10232646137860026239)
XLA Ops:
  1.3 32.7 %step.1 = (f32[5,8,8,128]{3,2,1,0:T(8,128)S(1)}, f32[16,16,128]{2,1,0:T(8,128)S(1)}, bf16[80,256]{1,0:T(8,128)(2,1)S(1)}) custom-call(f32[5,16,8,128]{3,2,1,0:T(8,128)} %state_in.1, s32[5,1,1,16]{3,2,1,0:T(1,128)} %counts_in.1, s32[1,1]{1,0:T(1,128)} %bitcast.2.agg_in, bf16[112,320]{1,0:T(8,128)(2,1)} %constant.8.clone.first_in, ...), custom_call_target="tpu_custom_call" | custom-call | tf_op jit(solution)/shard_map/step/pallas_call | solution.py:561
  34.0 0.8 %place.1 = (f32[5,8,8,128]{3,2,1,0:T(8,128)}, f32[80,128]{1,0:T(8,128)}) custom-call(f32[5,8,8,128]{3,2,1,0:T(8,128)S(1)} %get-tuple-element.7.adv, f32[16,16,128]{2,1,0:T(8,128)S(1)} %get-tuple-element.8.ga, bf16[80,256]{1,0:T(8,128)(2,1)S(1)} %get-tuple-element.9.pick), custom_call_target="tpu_custom_call" | custom-call | tf_op jit(solution)/shard_map/place/pallas_call | solution.py:606

commit v6 on v5

--- a/solution.py
+++ b/solution.py
@@ -333,86 +333,6 @@
     maxsend[1] = jnp.where(lane1 < 64, best, rollto(best, 64, 1))
     send(maxsend.at[1], rw, w_of, far_w, sem_w)
 
-    all_q.wait_recv()
-    all_h.wait_recv()
-    for f in range(5):
-        for k in range(6):
-            a, b = recvx[0, f, k], recvx[1, f, k]
-            XH[f, k] = jnp.where(row8 < 4, a, rollto(b, 4, 0))
-            XH[f, k + 6] = jnp.where(row8 < 4, rollto(a, 4, 0), b)
-    for z in range(12):
-        w = prims_of([XH[f, z] for f in range(5)])
-        for f in range(5):
-            Wx[f, z] = w[f]
-    colm = iota((8, 128), 1) % 8
-    packed = []
-    for f in range(5):
-        q = qown[f]
-        qh = pack_columns(lambda z: XH[f, z - 2], range(2, 14))
-        lo = jnp.where(row8 < 4, recvq[2, f], recvq[3, f])
-        hi = jnp.where(row8 < 4, recvq[4, f], recvq[5, f])
-        packed.append(
-            jnp.stack(
-                [
-                    jnp.where(colm < 4, recvq[0, f], q),
-                    jnp.where(colm < 4, q, recvq[1, f]),
-                    jnp.where(colm < 4, lo, qh),
-                    jnp.where(colm < 4, qh, hi),
-                ]
-            )
-        )
-    pw = prims_of(packed)
-    pr, pf = packed_y(pw)
-    ta, _ = x_terms([x[:2] for x in pw], [x[2:] for x in pw])
-    tz = packed_z([x[:2] for x in pw])
-    for f in range(5):
-        ty = pf[f] - rollto(pf[f], 1, 2)
-        qx[0, f] = packed[f][:2]
-        qx[1, f] = ta[f] + tz[f] + ty[:2]
-
-    def inject(e1, e2, pw, pr, pf, low, high, planes, offset):
-        for f in range(5):
-            c1 = edge_lanes(pw[f][low], pw[f][high])
-            c2 = edge_lanes(pf[f][low], pr[f][high])
-            for z in planes:
-                e1[f, z - offset] = rollto(c1, -(8 * z + 8), 1)
-                e2[f, z - offset] = rollto(c2, -(8 * z + 8), 1)
-
-    inject(E1, E2, pw, pr, pf, 0, 1, range(2, 14), 2)
-    inject(E1x, E2x, pw, pr, pf, 2, 3, range(4, 12), 4)
-
-    def xy_main(i, carry):
-        z0 = i * PAIR
-        a = load(W, z0 + 2, PAIR)
-        ta, tb = x_terms(a, load(Wx, z0, PAIR))
-        ty = y_term(a, load(E1, z0, PAIR), load(E2, z0, PAIR))
-        for f in range(5):
-            L[f, pl.ds(z0, PAIR)] = L[f, pl.ds(z0, PAIR)] + ta[f] + ty[f]
-            Lx[f, pl.ds(z0, PAIR)] = tb[f]
-        return carry
-
-    lax.fori_loop(0, 12 // PAIR, xy_main, 0)
-
-    def strip(i, carry):
-        z0 = i * PAIR
-        w = load(Wx, z0, PAIR + 4)
-        tz = z_term(w)
-        ty = y_term([x[2:-2] for x in w], load(E1x, z0, PAIR), load(E2x, z0, PAIR))
-        for f in range(5):
-            Lx[f, pl.ds(z0 + 2, PAIR)] = Lx[f, pl.ds(z0 + 2, PAIR)] + tz[f] + ty[f]
-        return carry
-
-    lax.fori_loop(0, 8 // PAIR, strip, 0)
-    for f in range(5):
-        for j, r in enumerate((6, 7, 0, 1)):
-            for z in range(8):
-                xedge[0, f, j, z : z + 1, :] = XH[f, z + 2, r : r + 1, :]
-                xedge[1, f, j, z : z + 1, :] = Lx[f, z + 2, r : r + 1, :]
-        for j, r in enumerate((0, 1, 7)):
-            for z in range(8):
-                xedge[0, f, j + 4, z : z + 1, :] = state[f, z + 4, r : r + 1, :]
-                xedge[1, f, j + 4, z : z + 1, :] = L[f, z + 2, r : r + 1, :]
-
     leader = agg[...]
     me_rank = (gy - leader + ngy) & (ngy - 1)
     nlane = ngy * 16
@@ -454,6 +374,86 @@
     in_row = q - (starts >> 7)
     pick[...] = jnp.where((in_row == iota((nrow, nlane), 1) % 16) & lead, 1.0, 0.0).astype(BF16)
     ga[:, 10:16] = jnp.zeros((ngy, 6, 128), F32)
+
+    all_q.wait_recv()
+    all_h.wait_recv()
+    for f in range(5):
+        for k in range(6):
+            a, b = recvx[0, f, k], recvx[1, f, k]
+            XH[f, k] = jnp.where(row8 < 4, a, rollto(b, 4, 0))
+            XH[f, k + 6] = jnp.where(row8 < 4, rollto(a, 4, 0), b)
+    for z in range(12):
+        w = prims_of([XH[f, z] for f in range(5)])
+        for f in range(5):
+            Wx[f, z] = w[f]
+    colm = iota((8, 128), 1) % 8
+    packed = []
+    for f in range(5):
+        q = qown[f]
+        qh = pack_columns(lambda z: XH[f, z - 2], range(2, 14))
+        lo = jnp.where(row8 < 4, recvq[2, f], recvq[3, f])
+        hi = jnp.where(row8 < 4, recvq[4, f], recvq[5, f])
+        packed.append(
+            jnp.stack(
+                [
+                    jnp.where(colm < 4, recvq[0, f], q),
+                    jnp.where(colm < 4, q, recvq[1, f]),
+                    jnp.where(colm < 4, lo, qh),
+                    jnp.where(colm < 4, qh, hi),
+                ]
+            )
+        )
+    pw = prims_of(packed)
+    pr, pf = packed_y(pw)
+    ta, _ = x_terms([x[:2] for x in pw], [x[2:] for x in pw])
+    tz = packed_z([x[:2] for x in pw])
+    for f in range(5):
+        ty = pf[f] - rollto(pf[f], 1, 2)
+        qx[0, f] = packed[f][:2]
+        qx[1, f] = ta[f] + tz[f] + ty[:2]
+
+    def inject(e1, e2, pw, pr, pf, low, high, planes, offset):
+        for f in range(5):
+            c1 = edge_lanes(pw[f][low], pw[f][high])
+            c2 = edge_lanes(pf[f][low], pr[f][high])
+            for z in planes:
+                e1[f, z - offset] = rollto(c1, -(8 * z + 8), 1)
+                e2[f, z - offset] = rollto(c2, -(8 * z + 8), 1)
+
+    inject(E1, E2, pw, pr, pf, 0, 1, range(2, 14), 2)
+    inject(E1x, E2x, pw, pr, pf, 2, 3, range(4, 12), 4)
+
+    def xy_main(i, carry):
+        z0 = i * PAIR
+        a = load(W, z0 + 2, PAIR)
+        ta, tb = x_terms(a, load(Wx, z0, PAIR))
+        ty = y_term(a, load(E1, z0, PAIR), load(E2, z0, PAIR))
+        for f in range(5):
+            L[f, pl.ds(z0, PAIR)] = L[f, pl.ds(z0, PAIR)] + ta[f] + ty[f]
+            Lx[f, pl.ds(z0, PAIR)] = tb[f]
+        return carry
+
+    lax.fori_loop(0, 12 // PAIR, xy_main, 0)
+
+    def strip(i, carry):
+        z0 = i * PAIR
+        w = load(Wx, z0, PAIR + 4)
+        tz = z_term(w)
+        ty = y_term([x[2:-2] for x in w], load(E1x, z0, PAIR), load(E2x, z0, PAIR))
+        for f in range(5):
+            Lx[f, pl.ds(z0 + 2, PAIR)] = Lx[f, pl.ds(z0 + 2, PAIR)] + tz[f] + ty[f]
+        return carry
+
+    lax.fori_loop(0, 8 // PAIR, strip, 0)
+    for f in range(5):
+        for j, r in enumerate((6, 7, 0, 1)):
+            for z in range(8):
+                xedge[0, f, j, z : z + 1, :] = XH[f, z + 2, r : r + 1, :]
+                xedge[1, f, j, z : z + 1, :] = Lx[f, z + 2, r : r + 1, :]
+        for j, r in enumerate((0, 1, 7)):
+            for z in range(8):
+                xedge[0, f, j + 4, z : z + 1, :] = state[f, z + 4, r : r + 1, :]
+                xedge[1, f, j + 4, z : z + 1, :] = L[f, z + 2, r : r + 1, :]
 
     all_w.wait_recv()
     best = maxsend[1]

time: 34.9 us -> 34.8 us (level)
  no operation moved by 1% of the time
where the time goes in v6:
time: 34.8 us; the launch traced here: 34.7 us
  Pallas kernels  33.4 us (96%)
  between operations  1.28 us (4%)
    pallas_call x1, Pallas kernels, shards(): pl.pallas_call(functools.partial(kernel, ngx, ngy), out_shape=(vm((5, 8,...  32.6 us
    pallas_call x1, Pallas kernels, shards(): pl.pallas_call(place, out_shape=(jax.ShapeDtypeStruct(adv.shape, F32), ja...  0.8 us

profile of v6, /device:TPU:1, one launch (start us, length us, event | category | flops | bytes accessed | tf_op | source)
XLA Modules:
  0.0 34.7 jit_solution(9349882194059997767)
XLA Ops:
  1.3 32.6 %step.1 = (f32[5,8,8,128]{3,2,1,0:T(8,128)S(1)}, f32[16,16,128]{2,1,0:T(8,128)S(1)}, bf16[80,256]{1,0:T(8,128)(2,1)S(1)}) custom-call(f32[5,16,8,128]{3,2,1,0:T(8,128)} %state_in.1, s32[5,1,1,16]{3,2,1,0:T(1,128)} %counts_in.1, s32[1,1]{1,0:T(1,128)} %bitcast.2.agg_in, bf16[112,320]{1,0:T(8,128)(2,1)} %constant.8.clone.first_in, ...), custom_call_target="tpu_custom_call" | custom-call | tf_op jit(solution)/shard_map/step/pallas_call | solution.py:561
  33.9 0.8 %place.1 = (f32[5,8,8,128]{3,2,1,0:T(8,128)}, f32[80,128]{1,0:T(8,128)}) custom-call(f32[5,8,8,128]{3,2,1,0:T(8,128)S(1)} %get-tuple-element.7.adv, f32[16,16,128]{2,1,0:T(8,128)S(1)} %get-tuple-element.8.ga, bf16[80,256]{1,0:T(8,128)(2,1)S(1)} %get-tuple-element.9.pick), custom_call_target="tpu_custom_call" | custom-call | tf_op jit(solution)/shard_map/place/pallas_call | solution.py:606
